TPU v7x, 512 devices: a whole 4x4x16 slice. The times are simulated.
512 devices in a mesh: fsdp: 128 (over y, z_lo, x), dp: 4 (over z_hi, core).
Axes of the slice: x: 4, y: 4, z: 16 (z_hi: 2, z_lo: 8; z = z_hi * 8 + z_lo), core: 2. Of those that a mesh axis runs over, the one named last changes fastest.
Arguments:
- tokens: bfloat16 [65536, 4096], P(('fsdp', 'dp')), may hold values from -6 to 6
- norm_gain: float32 [4096], replicated, may hold values from 0.25 to 1.75
- penalty: float32 [14336], P('dp'), may hold values from 0.25 to 4
- weight_tiles: bfloat16 [4, 384, 4096], P(None, 'fsdp'), may hold values from -0.375 to 0.375
- block_rows: int32 [224, 4], replicated, may hold values from 0 to 63, as said below
- block_slot: int32 [224, 4], replicated, may hold values from 0 to 383, as said below
Outputs:
- grad_tokens: bfloat16 [65536, 4096], P(('fsdp', 'dp'))
Inputs may be any that keep to these rules, and one draw needn't show every extreme that they name: `block_rows`: each block column names 4 distinct block rows. Within each run of 56 block columns (columns q * 56 to (q + 1) * 56 - 1), a block row is named at most 4 times, and some block row exactly 4 times. `block_slot`: within each run of 56 block columns, no slot is named twice. Slot s is stored by fsdp index s // 3; in each run some fsdp index has all 3 of its slots named.
All inputs are finite; a program needn't handle non-finite values.
Results may differ from a plain program's by a relative error of at most 0.014.
Values may be sent and summed in bfloat16 or wider, within the bound.
No kernel may reach another device: no remote copies, remote signals or barrier semaphores. Data moves between devices by JAX's collectives and lax.ppermute only.
A program may use at most 128 MiB of HBM per device.

v0:
```python
import math

import jax
import jax.numpy as jnp
from jax import lax
from jax.sharding import PartitionSpec as P

BLOCK = 64


def on_device(tokens, norm_gain, penalty, weight_tiles, block_rows, block_slot):
    quarter = lax.axis_index("dp")
    model_width = tokens.shape[1]
    as_float = tokens.astype(jnp.float32)
    rms_scale = jnp.sqrt(jnp.mean(as_float * as_float, axis=1, keepdims=True) + 1e-05)
    normed = as_float / rms_scale
    scaled = (normed * norm_gain).astype(jnp.bfloat16)
    own_tiles = lax.dynamic_index_in_dim(weight_tiles, quarter, 0, keepdims=False)
    gathered = lax.all_gather(scaled, "dp", axis=0, tiled=True)
    group_rows = gathered.shape[0]
    row_blocks = model_width // BLOCK
    per_column = block_rows.shape[1]
    col_blocks = penalty.shape[0] // BLOCK
    rows_here = lax.dynamic_slice_in_dim(block_rows, quarter * col_blocks, col_blocks, 0)
    slots_here = lax.dynamic_slice_in_dim(block_slot, quarter * col_blocks, col_blocks, 0)
    entries = col_blocks * per_column
    flat_slots = slots_here.reshape(-1)
    stored = lax.all_gather(own_tiles, "fsdp", axis=0, tiled=True)
    weights_here = stored[flat_slots].reshape(entries, BLOCK, BLOCK)
    feat_blocks = gathered.T.reshape(row_blocks, BLOCK, group_rows)
    unit_scale = penalty.reshape(col_blocks, BLOCK, 1)
    col_size = math.gcd(col_blocks, 4)
    col_groups = col_blocks // col_size

    def forward_group(pieces):
        weight_group, row_group, unit_group = pieces
        selected = feat_blocks[row_group]
        preact = jnp.einsum(
            "gkio,gkin->gon", weight_group, selected, preferred_element_type=jnp.float32
        )
        gating = jax.nn.sigmoid(preact)
        grad_act = unit_group * (preact * gating)
        grad_pre = grad_act * (gating * (1.0 + preact * (1.0 - gating)))
        return grad_pre.astype(jnp.bfloat16)

    grad_pre = lax.map(
        forward_group,
        (
            weights_here.reshape(col_groups, col_size, per_column, BLOCK, BLOCK),
            rows_here.reshape(col_groups, col_size, per_column),
            unit_scale.reshape(col_groups, col_size, BLOCK, 1),
        ),
    )
    grad_pre = grad_pre.reshape(col_blocks, BLOCK, group_rows)
    row_cap = -(-entries // row_blocks)
    flat_rows = rows_here.reshape(-1)
    row_hits = (flat_rows[:, None] == jnp.arange(row_blocks, dtype=jnp.int32)[None, :]).astype(
        jnp.int32
    )
    hits_before = jnp.cumsum(row_hits, axis=0) - row_hits
    row_rank = jnp.sum(hits_before * row_hits, axis=1)
    slot_table = jnp.full((row_blocks * row_cap,), entries, jnp.int32)
    slot_table = slot_table.at[flat_rows * row_cap + row_rank].set(
        jnp.arange(entries, dtype=jnp.int32)
    )
    padded_tiles = jnp.concatenate([weights_here, jnp.zeros((1, BLOCK, BLOCK), jnp.bfloat16)], 0)
    back_tiles = padded_tiles[slot_table].reshape(row_blocks, row_cap, BLOCK, BLOCK)
    back_columns = jnp.where(slot_table < entries, slot_table // per_column, 0).reshape(
        row_blocks, row_cap
    )
    row_size = math.gcd(row_blocks, 4)
    row_groups = row_blocks // row_size
    grad_part = grad_pre

    def one_group(pieces):
        tile_group, column_group = pieces
        selected = grad_part[column_group]
        return jnp.einsum(
            "gqio,gqon->ngi", tile_group, selected, preferred_element_type=jnp.float32
        )

    grouped = lax.map(
        one_group,
        (
            back_tiles.reshape(row_groups, row_size, row_cap, BLOCK, BLOCK),
            back_columns.reshape(row_groups, row_size, row_cap),
        ),
    )
    summed = lax.psum_scatter(
        grouped.transpose(1, 0, 2, 3).reshape(group_rows, model_width).astype(jnp.bfloat16),
        "dp",
        scatter_dimension=0,
        tiled=True,
    ).astype(jnp.float32)
    grad_norm = summed * norm_gain
    mixing = jnp.mean(grad_norm * normed, axis=1, keepdims=True)
    return ((grad_norm - normed * mixing) / rms_scale).astype(jnp.bfloat16)


def solution(mesh):
    placed = (P(("fsdp", "dp"), None), P(), P("dp"), P(None, "fsdp", None), P(), P())
    return jax.shard_map(
        on_device, mesh=mesh, in_specs=placed, out_specs=P(("fsdp", "dp"), None), check_vma=False
    )
```

profile of v0, /device:TPU:1, one launch (start us, length us, event | category | flops | bytes accessed | tf_op | source)
XLA Modules:
  0.0 1400.3 jit_solution(17715397416254381017)
XLA Ops:
  10.4 2.2 multiply_convert_fusion.1
  16.2 877.6 %all-gather.6.cloned.1.call-done = bf16[1,384,4096]{2,0,1:T(2,128)(2,1)} async-done(((bf16[1,3,4096]{2,0,1:T(2,128)(2,1)}), bf16[1,384,4096]{2,0,1:T(2,128)(2,1)}) %all-gather.6.cloned.1.call-update) | async-done | bytes 3145744 | tf_op jit(solution)/shard_map/all_gather | solution.py:28
  893.8 6.3 copy.69
  900.2 2.9 gather_fusion.2
  903.1 4.1 copy.55
  907.2 4.9 reshape_reshape.14
  912.1 5.6 copy.56
  917.8 4.9 concatenate.3
  922.6 5.1 gather_fusion.3
  927.7 174.2 %all-gather.4.cloned.1.call-done = bf16[512,4096]{0,1:T(8,128)(2,1)} async-done(((bf16[128,4096]{0,1:T(8,128)(2,1)}), bf16[512,4096]{0,1:T(8,128)(2,1)}) %all-gather.4.cloned.1.call-update) | async-done | bytes 4194320 | tf_op jit(solution)/shard_map/all_gather | solution.py:19
  1101.9 70.7 %while.20 = (s32[]{:T(128)}, bf16[14,4,64,512]{3,2,1,0:T(8,128)(2,1)}, f32[14,4,64,1]{2,1,3,0:T(4,128)S(1)}, bf16[14,4,4,64,64]{4,3,2,1,0:T(8,128)(2,1)}, s32[14...) while((s32[]{:T(128)}, bf16[14,4,64,512]{3,2,1,0:T(8,128)(2,1)}, ...), condition=%wide.region_6.7_spmd, body=%wide.region_5.6_spmd.sunk | while | flops 68551728 | bytes 3678677 | solution.py:46
  1102.0 2.8 gather_fusion
  1104.9 2.1 fusion.24
  1107.1 2.8 gather_fusion
  1109.9 2.1 fusion.24
  1112.2 2.8 gather_fusion
  1115.0 2.1 fusion.24
  1117.2 2.8 gather_fusion
  1120.0 2.1 fusion.24
  1122.3 2.8 gather_fusion
  1125.1 2.1 fusion.24
  1127.3 2.8 gather_fusion
  1130.1 2.1 fusion.24
  1132.3 2.8 gather_fusion
  1135.2 2.1 fusion.24
  1137.4 2.8 gather_fusion
  1140.2 2.1 fusion.24
  1142.4 2.8 gather_fusion
  1145.3 2.1 fusion.24
  1147.5 2.8 gather_fusion
  1150.3 2.1 fusion.24
  1152.5 2.8 gather_fusion
  1155.3 2.1 fusion.24
  1157.5 2.8 gather_fusion
  1160.4 2.1 fusion.24
  1162.6 2.8 gather_fusion
  1165.4 2.1 fusion.24
  1167.7 2.8 gather_fusion
  1170.5 2.1 fusion.24
  1172.6 76.2 %while.21 = (s32[]{:T(128)}, bf16[16,512,4,64]{1,3,2,0:T(8,128)(2,1)}, s32[16,4,4]{2,1,0:T(4,128)S(1)}, bf16[56,64,512]{2,1,0:T(8,128)(2,1)}, bf16[16,4,4,64,64]{4,3,2,1,0:T(8,128)(2,1)}, /*index=5*/s32[]{:T(128)}) while((s32[]{:T(128)}, bf16[16,512,4,64]{1,3,2,0:T(8,128)(2,1)}, s32[16,4,4]{2,1,0:T(4,128)S(1)}, ...), condition=%wide.region_8.9_spmd, body=%wide.region_7.8_spmd.sunk | while | flops 67109936 | bytes 3937737 | solution.py:82
  1172.7 2.7 gather_fusion.1
  1177.5 2.7 gather_fusion.1
  1182.2 2.7 gather_fusion.1
  1184.9 2.0 fusion.27
  1187.0 2.7 gather_fusion.1
  1191.8 2.7 gather_fusion.1
  1196.5 2.7 gather_fusion.1
  1201.3 2.7 gather_fusion.1
  1206.0 2.7 gather_fusion.1
  1208.7 2.0 fusion.27
  1210.8 2.7 gather_fusion.1
  1215.5 2.7 gather_fusion.1
  1220.3 2.7 gather_fusion.1
  1223.0 2.0 fusion.27
  1225.1 2.7 gather_fusion.1
  1227.7 2.0 fusion.27
  1229.8 2.7 gather_fusion.1
  1234.6 2.7 gather_fusion.1
  1237.3 2.0 fusion.27
  1239.4 2.7 gather_fusion.1
  1242.0 2.0 fusion.27
  1244.1 2.7 gather_fusion.1
  1248.8 6.4 copy.60
  1255.3 134.1 %reduce-scatter.4.cloned.1.call-done = bf16[128,4096]{1,0:T(8,128)(2,1)} async-done(((bf16[512,4096]{1,0:T(8,128)(2,1)}), bf16[128,4096]{1,0:T(8,128)(2,1)}) %reduce-scatter.4.cloned.1.call-update) | async-done | bytes 1048592
  (171 shorter events, 34.7 us)
Async XLA Ops:
  6.5 0.9 copy-start
  6.5 6.1 copy-start.6
  6.5 7.5 copy-start.7
  6.5 7.8 copy-start.5
  6.5 887.3 %all-gather.6.cloned.1.call-start = ((), (), s32[]{:S(2)}) async-start(), calls=%async_computation.2 | async-start | bytes 6340608 | tf_op jit(solution)/shard_map/all_gather | solution.py:28
  8.1 1093.8 %all-gather.4.cloned.1.call-start = ((), (), s32[]{:S(2)}) async-start(), calls=%async_computation.1 | async-start | bytes 5242880 | tf_op jit(solution)/shard_map/all_gather | solution.py:19
  9.8 6.4 copy-start.1
  12.6 1376.8 %reduce-scatter.4.cloned.1.call-start = ((), (), s32[]{:S(2)}) async-start(), calls=%async_computation.3 | async-start | bytes 5242880
  903.1 4.1 copy-start.3
  1255.2 135.8 %copy-start.2 = (bf16[128,4096]{0,1:T(8,128)(2,1)S(1)}, bf16[128,4096]{0,1:T(8,128)(2,1)}, u32[]{:S(2)}) copy-start(bf16[128,4096]{0,1:T(8,128)(2,1)} %copy-done.1) | copy-start | bytes 3145732
  1255.2 135.8 %copy-start.4 = (f32[4096]{0:T(1024)S(1)}, f32[4096]{0:T(1024)}, u32[]{:S(2)}) copy-start(f32[4096]{0:T(1024)} %param.11) | copy-start | bytes 49156
Sparse Core Ops, SparseCore 0:
  9.4 884.3 all-gather.5
  895.9 205.9 all-gather.3
  1255.4 133.9 reduce-scatter.3
where the time goes:
time: 1400 us
  waiting for transfers between devices  1190 us (85%)
  local copies, waits for them, and re-layouts  133 us (10%)
  matrix products  61.8 us (4%)
    all_gather x1, waiting for transfers between devices, on_device(): stored = lax.all_gather(own_tiles, 'fsdp', axis=0, tiled=True)  878 us
    all_gather x1, waiting for transfers between devices, on_device(): gathered = lax.all_gather(scaled, 'dp', axis=0, tiled=True)  174 us
    unnamed x4, waiting for transfers between devices  134 us
    gather x16, local copies, waits for them, and re-layouts, one_group(): selected = grad_part[column_group]  42.4 us
    gather x14, local copies, waits for them, and re-layouts, forward_group(): selected = feat_blocks[row_group]  39.2 us
    dot_general x16, matrix products, one_group(): jnp.einsum('gqio,gqon->ngi', tile_group, selected, preferred_element_type...  32.1 us
    dot_general x14, matrix products, forward_group(): jnp.einsum('gkio,gkin->gon', weight_group, selected, preferred_element_ty...  29.7 us
  transfers between devices with their start and end apart: 3, of which 3 were waited for; matrix products, arithmetic and copies ran while one was open for 3% of the time, Pallas kernels for 0%

commit v1 on v0

v1 whole, which is shorter than its diff:
```python
import jax
import jax.numpy as jnp
from jax import lax
from jax.experimental import pallas as pl
from jax.experimental.pallas import tpu as pltpu
from jax.sharding import Mesh
from jax.sharding import PartitionSpec as P

BLOCK = 64
HALF = BLOCK // 2
EPS = 1e-05
LANES = 128
GROUP = 8
NX, NY, NZ = 4, 4, 8
SIDE = 4
AXES = ("y", "zl", "x", "zh", "core")


def norm_kernel(tokens_ref, gain_ref, feat_ref, inverse_ref):
    x = tokens_ref[...].astype(jnp.float32)
    inverse = 1.0 / jnp.sqrt(jnp.mean(x * x, axis=1, keepdims=True) + EPS)
    inverse_ref[...] = inverse
    scaled = ((x * inverse) * gain_ref[...]).astype(jnp.bfloat16)
    for at in range(0, x.shape[1], LANES):
        feat_ref[at : at + LANES, :] = scaled[:, at : at + LANES].T


def sparse_kernel(columns, per_column, pieces, refs):
    tile_ref, row_ref, unit_ref, mine_ref, other_ref = refs[:5]
    parts = refs[5 : 5 + len(pieces)]
    keep_ref, send_ref, away_ref, w_ref, sems = refs[5 + len(pieces) :]
    count = mine_ref.shape[2]

    copies = []
    for i, (run, start, size) in enumerate(pieces):
        copies.append(
            pltpu.make_async_copy(parts[i], w_ref.at[run, pl.ds(start, size)], sems.at[i])
        )
    for copy in copies:
        copy.start()
    keep_ref[...] = jnp.zeros_like(keep_ref)
    away_ref[...] = jnp.zeros_like(away_ref)
    blank = jnp.zeros((BLOCK, 2 * count), jnp.bfloat16)

    def work(run):
        def group(g, carry):
            first = (run * columns + g * GROUP) * per_column
            units = unit_ref[run, g]

            def forward(j):
                at = first + j * per_column
                rows = [row_ref[at + k] for k in range(per_column)]
                stack = jnp.concatenate(
                    [w_ref[run, tile_ref[at + k]] for k in range(per_column)], axis=0
                )
                turned = stack.T
                lhs = jnp.concatenate([turned[:BLOCK], turned[BLOCK:]], axis=1)
                mine = [mine_ref[r] for r in rows]
                other = [other_ref[r] for r in rows]
                rhs = jnp.concatenate(
                    [
                        jnp.concatenate([p[:HALF] for p in side] + [p[HALF:] for p in side], axis=0)
                        for side in (mine, other)
                    ],
                    axis=1,
                )
                preact = jnp.dot(lhs, rhs, preferred_element_type=jnp.float32)
                gating = jax.nn.sigmoid(preact)
                grad_act = units[:, j : j + 1] * (preact * gating)
                grad_pre = grad_act * (gating * (1.0 + preact * (1.0 - gating)))
                return rows, stack, grad_pre.astype(jnp.bfloat16)

            def backward(rows, stack, grad_pre):
                upper = jnp.dot(
                    stack,
                    jnp.concatenate([grad_pre, blank], axis=0),
                    preferred_element_type=jnp.float32,
                )
                lower = jnp.dot(
                    stack,
                    jnp.concatenate([blank, grad_pre], axis=0),
                    preferred_element_type=jnp.float32,
                )
                for ref, lanes in ((keep_ref, slice(0, count)), (away_ref, slice(count, None))):
                    sums = []
                    for k in range(per_column):
                        span = slice(k * HALF, (k + 1) * HALF)
                        term = jnp.concatenate([upper[span, lanes], lower[span, lanes]], axis=0)
                        sums.append(ref[rows[k]] + term)
                    for k in range(per_column):
                        ref[rows[k]] = sums[k]

            held = [forward(j) for j in range(GROUP)]
            for piece in held:
                backward(*piece)
            return carry

        lax.fori_loop(0, columns // GROUP, group, 0)

    for run in range(2):
        for copy, piece in zip(copies, pieces):
            if piece[0] == run:
                copy.wait()
        work(run)
    send_ref[...] = away_ref[...].astype(jnp.bfloat16)


def close_kernel(keep_ref, came_ref, tokens_ref, gain_ref, inverse_ref, out_ref, grad_ref):
    inverse = inverse_ref[...]
    width = tokens_ref.shape[1]
    total = jnp.zeros((tokens_ref.shape[0], LANES), jnp.float32)
    for at in range(0, width, LANES):
        span = slice(at, at + LANES)
        grad = (keep_ref[span, :] + came_ref[span, :].astype(jnp.float32)).T
        grad = grad * gain_ref[:, span]
        grad_ref[:, span] = grad
        total += grad * (tokens_ref[:, span].astype(jnp.float32) * inverse)
    mixing = jnp.sum(total, axis=1, keepdims=True) * (1.0 / width)
    for at in range(0, width, LANES):
        span = slice(at, at + LANES)
        normed = tokens_ref[:, span].astype(jnp.float32) * inverse
        out_ref[:, span] = ((grad_ref[:, span] - normed * mixing) * inverse).astype(jnp.bfloat16)


def along_z(v, step):
    size = 2 * NZ
    at = lambda z: (z % NZ) * 2 + z // NZ
    return lax.ppermute(v, ("zl", "zh"), [(at(z), at((z + step) % size)) for z in range(size)])


def along_side(v, step, leg):
    pairs = []
    for y in range(NY):
        for x in range(NX):
            for core in range(2):
                to_y, to_x = (y, (x + step) % NX) if core == leg else ((y + step) % NY, x)
                pairs.append(((y * NX + x) * 2 + core, (to_y * NX + to_x) * 2 + core))
    return lax.ppermute(v, ("y", "x", "core"), pairs)


def swap_cores(v):
    return lax.ppermute(v, "core", [(0, 1), (1, 0)])


def gather_tiles(own):
    slots = own.shape[1]
    own = own[:, None]
    below, above = along_z(own, 1), along_z(own, -1)
    near = jnp.concatenate([below, own, above], axis=1)
    far_below = along_z(near, 3)
    far_above = along_z(near[:, :2], -3)
    line = jnp.concatenate([own, above, far_above, far_below, below], axis=1)
    line = line.reshape(2, NZ * slots, HALF, 2 * BLOCK)
    back, ahead = along_side(line, 1, 0), along_side(line, -1, 0)
    across = (along_side(back[0], 1, 0), along_side(ahead[1], -1, 0))
    found = []
    for run in range(2):
        plane = jnp.concatenate([line[run], ahead[run], across[run], back[run]], axis=0)
        found.append((plane, along_side(plane, 1, 1), along_side(plane, -1, 1)))
    pieces, arrays = [], []
    for run, (plane, back, ahead) in enumerate(found):
        size = plane.shape[0]
        half = size // 2
        from_back = along_side(back[:half], 1, 1)
        from_ahead = along_side(ahead[half:], -1, 1)
        pieces += [
            (run, 0, size),
            (run, size, size),
            (run, 2 * size, half),
            (run, 2 * size + half, half),
            (run, 3 * size, size),
        ]
        arrays += [plane, ahead, from_back, from_ahead, back]
    return pieces, arrays


def tile_places(block_slot, slots, y, zl, x, core):
    owner, place = block_slot // slots, block_slot % slots
    step_x = (owner % NX - x) % NX
    step_z = ((owner // NX) % NZ - zl) % NZ
    step_y = (owner // (NX * NZ) - y) % NY
    first = jnp.where(core == 0, step_x, step_y)
    second = jnp.where(core == 0, step_y, step_x)
    return ((second * SIDE + first) * NZ + step_z) * slots + place


def sparse_call(places, rows, units, mine, other, pieces, arrays):
    row_blocks, _, count = mine.shape
    columns, per_column = rows.shape[1:]
    tiles = SIDE * SIDE * NZ * (arrays[0].shape[0] // (SIDE * NZ))

    def body(*refs):
        sparse_kernel(columns, per_column, pieces, refs)

    smem = pl.BlockSpec(memory_space=pltpu.SMEM)
    vmem = pl.BlockSpec(memory_space=pltpu.VMEM)
    anywhere = pl.BlockSpec(memory_space=pl.ANY)
    return pl.pallas_call(
        body,
        out_shape=(
            jax.ShapeDtypeStruct((row_blocks, BLOCK, count), jnp.float32),
            jax.ShapeDtypeStruct((row_blocks, BLOCK, count), jnp.bfloat16),
        ),
        in_specs=[smem, smem, vmem, vmem, vmem] + [anywhere] * len(arrays),
        out_specs=(vmem, vmem),
        scratch_shapes=[
            pltpu.VMEM((row_blocks, BLOCK, count), jnp.float32),
            pltpu.VMEM((2, tiles, HALF, 2 * BLOCK), jnp.bfloat16),
            pltpu.SemaphoreType.DMA((len(arrays),)),
        ],
    )(places.reshape(-1), rows.reshape(-1), units, mine, other, *arrays)


def norm_call(tokens, gain):
    count, width = tokens.shape
    return pl.pallas_call(
        norm_kernel,
        out_shape=(
            jax.ShapeDtypeStruct((width, count), jnp.bfloat16),
            jax.ShapeDtypeStruct((count, 1), jnp.float32),
        ),
    )(tokens, gain)


def close_call(keep, came, tokens, gain, inverse):
    count, width = tokens.shape
    return pl.pallas_call(
        close_kernel,
        out_shape=jax.ShapeDtypeStruct((count, width), jnp.bfloat16),
        scratch_shapes=[pltpu.VMEM((count, width), jnp.float32)],
    )(keep.reshape(width, count), came.reshape(width, count), tokens, gain, inverse)


def unit_table(penalty, columns):
    return penalty.reshape(-1, columns // GROUP, GROUP, BLOCK).transpose(0, 1, 3, 2)


def pack_tiles(tiles):
    lead = tiles.shape[:-1]
    split = tiles.reshape(*lead, 2, HALF, BLOCK)
    return jnp.moveaxis(split, -3, -2).reshape(*lead, HALF, 2 * BLOCK)


def on_device(tokens, norm_gain, penalty, weight_tiles, block_rows, block_slot):
    y, zl, x, zh, core = (lax.axis_index(name) for name in AXES)
    runs, slots, tile_size = weight_tiles.shape
    count, width = tokens.shape
    columns, per_column = block_rows.shape[0] // runs, block_rows.shape[1]

    def of_core(table):
        paired = table.reshape(2, 2, *table.shape[1:])
        return lax.dynamic_index_in_dim(paired, core, 1, keepdims=False)

    own = pack_tiles(of_core(weight_tiles))
    pieces, arrays = gather_tiles(own)
    far_penalty = lax.ppermute(penalty, "zh", [(0, 1), (1, 0)])
    both = jnp.stack(
        [jnp.where(zh == 0, penalty, far_penalty), jnp.where(zh == 0, far_penalty, penalty)]
    )
    rows = of_core(block_rows.reshape(runs, columns, per_column))
    places = of_core(
        tile_places(block_slot, slots, y, zl, x, core).reshape(runs, columns, per_column)
    )
    gain = norm_gain.reshape(1, width)
    features, inverse = norm_call(tokens, gain)
    other = swap_cores(features)
    blocks = (width // BLOCK, BLOCK, count)
    keep, send = sparse_call(
        places, rows, unit_table(both, columns), features.reshape(blocks), other.reshape(blocks),
        pieces, arrays,
    )
    came = swap_cores(send)
    return close_call(keep, came, tokens, gain, inverse)


def solution(mesh):
    fine = Mesh(mesh.devices.reshape(NY, NZ, NX, 2, 2), AXES)
    placed = (P(AXES, None), P(), P(("zh", "core")), P(None, ("y", "zl", "x"), None), P(), P())
    return jax.shard_map(
        on_device, mesh=fine, in_specs=placed, out_specs=P(AXES, None), check_vma=False
    )
```

time: 1400 us -> 133 us (0.10)
  waiting for transfers between devices: 1190 us -> 19.2 us
  local copies, waits for them, and re-layouts: 133 us -> 11.3 us
  starting transfers between devices: 0.12 us -> 77 us
  matrix products: 61.8 us -> 0 us
  Pallas kernels: 0 us -> 22.5 us
    all_gather x2 -> x0, waiting for transfers between devices: 1050 us -> none  [the longest x1 878 us: on_device(): stored = lax.all_gather(own_tiles, 'fsdp', axis=0, tiled=True)]
    unnamed x4 -> x0, waiting for transfers between devices: 134 us -> none
    gather x33 -> x0, local copies, waits for them, and re-layouts: 93.8 us -> none  [the longest x16 42.4 us: one_group(): selected = grad_part[column_group]]
    ppermute x0 -> x19, starting transfers between devices: none -> 77 us  [the longest x12 39.7 us: along_side(): return lax.ppermute(v, ('y', 'x', 'core'), pairs)]
    dot_general x30 -> x0, matrix products: 61.8 us -> none  [the longest x16 32.1 us: one_group(): jnp.einsum('gqio,gqon->ngi', tile_group, selected, preferred_element_type...]
    pallas_call x0 -> x3, Pallas kernels: none -> 22.5 us  [the longest x1 15.3 us: sparse_call(): pl.pallas_call(body, out_shape=(jax.ShapeDtypeStruct((row_blocks, BLOCK,...]
    ppermute x0 -> x19, waiting for transfers between devices: none -> 19.2 us  [the longest x4 11.8 us: along_z(): lax.ppermute(v, ('zl', 'zh'), [(at(z), at((z + step) % size)) for z in ra...]
    unnamed x20 -> x29, local copies, waits for them, and re-layouts: 16.8 us -> 2.09 us
  transfers between devices with their start and end apart: 3 -> 19, of which waited for: 3 -> 7; matrix products, arithmetic and copies ran while one was open for 3% -> 7% of each run, Pallas kernels for 0% -> 2%
where the time goes in v1:
time: 133 us; the launch traced here: 132 us
  starting transfers between devices  77 us (58%)
  Pallas kernels  22.5 us (17%)
  waiting for transfers between devices  19.2 us (14%)
  local copies, waits for them, and re-layouts  11.3 us (8%)
    ppermute x12, starting transfers between devices, along_side(): return lax.ppermute(v, ('y', 'x', 'core'), pairs)  39.7 us
    ppermute x4, starting transfers between devices, along_z(): lax.ppermute(v, ('zl', 'zh'), [(at(z), at((z + step) % size)) for z in ra...  20.9 us
    pallas_call x1, Pallas kernels, sparse_call(): pl.pallas_call(body, out_shape=(jax.ShapeDtypeStruct((row_blocks, BLOCK,...  15.3 us
    ppermute x4, waiting for transfers between devices, along_z(): lax.ppermute(v, ('zl', 'zh'), [(at(z), at((z + step) % size)) for z in ra...  11.8 us
    ppermute x2, starting transfers between devices, swap_cores(): return lax.ppermute(v, 'core', [(0, 1), (1, 0)])  9.65 us
    ppermute x1, starting transfers between devices, on_device(): far_penalty = lax.ppermute(penalty, 'zh', [(0, 1), (1, 0)])  6.71 us
    ppermute x12, waiting for transfers between devices, along_side(): return lax.ppermute(v, ('y', 'x', 'core'), pairs)  4.91 us
    pallas_call x1, Pallas kernels, close_call(): pl.pallas_call(close_kernel, out_shape=jax.ShapeDtypeStruct((count, width...  4.34 us
  transfers between devices with their start and end apart: 19, of which 7 were waited for; matrix products, arithmetic and copies ran while one was open for 7% of the time, Pallas kernels for 2%

profile of v1, /device:TPU:1, one launch (start us, length us, event | category | flops | bytes accessed | tf_op | source)
XLA Modules:
  0.0 131.5 jit_solution(13946485349238057916)
XLA Ops:
  0.0 1.0 reshape.47
  1.0 0.1 constant_dynamic-slice_fusion
  1.1 0.1 copy.27
  1.2 0.1 reshape.48
  1.3 0.1 copy.23
  1.4 0.1 broadcast_in_dim_reshape.3
  1.5 4.4 %collective-permute-start.3 = (bf16[2,1,3,32,128]{4,3,2,0,1:T(8,128)(2,1)S(1)}, bf16[2,1,3,32,128]{4,3,2,0,1:T(8,128)(2,1)S(1)}, u32[]{:S(2)}, u32[]{:S(2)}) collective-permute-start(bf16[2,1,3,32,128]{4,3,2,0,1:T(8,128)(2,1)S(1)} %broadcast_in_dim_reshape.3), channel_id=1, source_target_pairs={{0,16},{16,32},{32,48},{48,64},{64,80},{80,96},{96,112},{112,2},{2... | collective-permute-start | bytes 147464 | tf_op jit(solution)/shard_map/ppermute | solution.py:128
  5.9 9.5 %collective-permute-start.2 = (bf16[2,1,3,32,128]{4,3,2,0,1:T(8,128)(2,1)S(1)}, bf16[2,1,3,32,128]{4,3,2,0,1:T(8,128)(2,1)S(1)}, u32[]{:S(2)}, u32[]{:S(2)}) collective-permute-start(bf16[2,1,3,32,128]{4,3,2,0,1:T(8,128)(2,1)S(1)} %broadcast_in_dim_reshape.3), channel_id=1, source_target_pairs={{0,114},{16,0},{32,16},{48,32},{64,48},{80,64},{96,80},{112,96},{2... | collective-permute-start | bytes 147464 | tf_op jit(solution)/shard_map/ppermute | solution.py:128
  15.4 0.0 collective-permute-done.3
  15.4 4.3 %collective-permute-start.4 = (bf16[2,2,3,32,128]{4,3,2,0,1:T(8,128)(2,1)S(1)}, bf16[2,2,3,32,128]{4,3,2,0,1:T(8,128)(2,1)S(1)}, u32[]{:S(2)}, u32[]{:S(2)}) collective-permute-start(bf16[2,2,3,32,128]{4,3,2,0,1:T(8,128)(2,1)S(1)} %pad_maximum_fusion.3), channel_id=1, source_target_pairs={{0,82},{16,98},{32,114},{48,0},{64,16},{80,32},{96,48},{112,64},{2... | collective-permute-start | bytes 294920 | tf_op jit(solution)/shard_map/ppermute | solution.py:128
  19.7 0.0 collective-permute-done.2
  19.7 2.8 %collective-permute-start.5 = (bf16[2,3,3,32,128]{4,3,2,0,1:T(8,128)(2,1)S(1)}, bf16[2,3,3,32,128]{4,3,2,0,1:T(8,128)(2,1)S(1)}, u32[]{:S(2)}, u32[]{:S(2)}) collective-permute-start(bf16[2,3,3,32,128]{4,3,2,0,1:T(8,128)(2,1)S(1)} %pad_maximum_fusion.2), channel_id=1, source_target_pairs={{0,48},{16,64},{32,80},{48,96},{64,112},{80,2},{96,18},{112,34},{2... | collective-permute-start | bytes 442376 | tf_op jit(solution)/shard_map/ppermute | solution.py:128
  22.6 0.4 collective-permute-done.4
  22.9 11.4 %collective-permute-done.5 = bf16[2,3,3,32,128]{4,3,2,0,1:T(8,128)(2,1)S(1)} collective-permute-done((bf16[2,3,3,32,128]{4,3,2,0,1:T(8,128)(2,1)S(1)}, bf16[2,3,3,32,128]{4,3,2,0,1:T(8,128)(2,1)S(1)}, u32[]{:S(2)}, u32[]{:S(2)}) %collective-permute-start.5) | collective-permute-done | bytes 147488 | tf_op jit(solution)/shard_map/ppermute | solution.py:128
  34.5 4.6 %collective-permute-start.6 = (bf16[2,24,32,128]{3,2,1,0:T(8,128)(2,1)S(1)}, bf16[2,24,32,128]{3,2,1,0:T(8,128)(2,1)S(1)}, u32[]{:S(2)}, u32[]{:S(2)}) collective-permute-start(bf16[2,24,32,128]{3,2,1,0:T(8,128)(2,1)S(1)} %bitcast.40), channel_id=1, source_target_pairs={{0,12},{1,385},{4,0},{5,389},{8,4},{9,393},{12,8},{13,397},{128,14... | collective-permute-start | bytes 1179656 | tf_op jit(solution)/shard_map/ppermute | solution.py:138
  39.1 1.9 %collective-permute-start.7 = (bf16[2,24,32,128]{3,2,1,0:T(8,128)(2,1)S(1)}, bf16[2,24,32,128]{3,2,1,0:T(8,128)(2,1)S(1)}, u32[]{:S(2)}, u32[]{:S(2)}) collective-permute-start(bf16[2,24,32,128]{3,2,1,0:T(8,128)(2,1)S(1)} %bitcast.41), channel_id=1, source_target_pairs={{0,4},{1,129},{4,8},{5,133},{8,12},{9,137},{12,0},{13,141},{128,13... | collective-permute-start | bytes 1179656 | tf_op jit(solution)/shard_map/ppermute | solution.py:138
  41.1 2.7 %collective-permute-done.6 = bf16[2,24,32,128]{3,2,1,0:T(8,128)(2,1)S(1)} collective-permute-done((bf16[2,24,32,128]{3,2,1,0:T(8,128)(2,1)S(1)}, bf16[2,24,32,128]{3,2,1,0:T(8,128)(2,1)S(1)}, u32[]{:S(2)}, u32[]{:S(2)}) %collective-permute-start.6) | collective-permute-done | bytes 393248 | tf_op jit(solution)/shard_map/ppermute | solution.py:138
  43.8 5.0 %collective-permute-start.13 = (bf16[24,32,128]{2,1,0:T(8,128)(2,1)S(1)}, bf16[24,32,128]{2,1,0:T(8,128)(2,1)S(1)}, u32[]{:S(2)}, u32[]{:S(2)}) collective-permute-start(bf16[24,32,128]{2,1,0:T(8,128)(2,1)S(1)} %get-tuple-element.15), channel_id=1, source_target_pairs={{0,12},{1,385},{4,0},{5,389},{8,4},{9,393},{12,8},{13,397},{128,14... | collective-permute-start | bytes 589832 | tf_op jit(solution)/shard_map/ppermute | solution.py:138
  48.9 0.3 collective-permute-done.7
  49.2 1.9 %collective-permute-start.8 = (bf16[24,32,128]{2,1,0:T(8,128)(2,1)S(1)}, bf16[24,32,128]{2,1,0:T(8,128)(2,1)S(1)}, u32[]{:S(2)}, u32[]{:S(2)}) collective-permute-start(bf16[24,32,128]{2,1,0:T(8,128)(2,1)S(1)} %get-tuple-element.18), channel_id=1, source_target_pairs={{0,4},{1,129},{4,8},{5,133},{8,12},{9,137},{12,0},{13,141},{128,13... | collective-permute-start | bytes 589832 | tf_op jit(solution)/shard_map/ppermute | solution.py:138
  51.1 0.4 collective-permute-done.13
  51.5 0.1 pad_maximum_fusion.1.refs_10_
  51.6 3.1 %collective-permute-start.15 = (bf16[96,32,128]{2,1,0:T(8,128)(2,1)S(1)}, bf16[96,32,128]{2,1,0:T(8,128)(2,1)S(1)}, u32[]{:S(2)}, u32[]{:S(2)}) collective-permute-start(bf16[96,32,128]{2,1,0:T(8,128)(2,1)S(1)} %pad_maximum_fusion.1.refs_10_), channel_id=1, source_target_pairs={{0,128},{1,5},{4,132},{5,9},{8,136},{9,13},{12,140},{13,1},{128,25... | collective-permute-start | bytes 2359304 | tf_op jit(solution)/shard_map/ppermute | solution.py:138
  54.7 3.5 %collective-permute-start.14 = (bf16[96,32,128]{2,1,0:T(8,128)(2,1)S(1)}, bf16[96,32,128]{2,1,0:T(8,128)(2,1)S(1)}, u32[]{:S(2)}, u32[]{:S(2)}) collective-permute-start(bf16[96,32,128]{2,1,0:T(8,128)(2,1)S(1)} %pad_maximum_fusion.1.refs_10_), channel_id=1, source_target_pairs={{0,384},{1,13},{4,388},{5,1},{8,392},{9,5},{12,396},{13,9},{128,0}... | collective-permute-start | bytes 2359304 | tf_op jit(solution)/shard_map/ppermute | solution.py:138
  58.2 0.0 collective-permute-done.8
  58.2 0.1 pad_maximum_fusion.refs_5_
  58.3 1.9 %collective-permute-start.10 = (bf16[96,32,128]{2,1,0:T(8,128)(2,1)S(1)}, bf16[96,32,128]{2,1,0:T(8,128)(2,1)}, u32[]{:S(2)}, u32[]{:S(2)}) collective-permute-start(bf16[96,32,128]{2,1,0:T(8,128)(2,1)S(1)} %pad_maximum_fusion.refs_5_), channel_id=1, source_target_pairs={{0,128},{1,5},{4,132},{5,9},{8,136},{9,13},{12,140},{13,1},{128,25... | collective-permute-start | bytes 2359304 | tf_op jit(solution)/shard_map/ppermute | solution.py:138
  60.3 4.6 %collective-permute-start.9 = (bf16[96,32,128]{2,1,0:T(8,128)(2,1)S(1)}, bf16[96,32,128]{2,1,0:T(8,128)(2,1)}, u32[]{:S(2)}, u32[]{:S(2)}) collective-permute-start(bf16[96,32,128]{2,1,0:T(8,128)(2,1)S(1)} %pad_maximum_fusion.refs_5_), channel_id=1, source_target_pairs={{0,384},{1,13},{4,388},{5,1},{8,392},{9,5},{12,396},{13,9},{128,0}... | collective-permute-start | bytes 2359304 | tf_op jit(solution)/shard_map/ppermute | solution.py:138
  64.9 2.8 %shard_map.64 = (bf16[4096,128]{1,0:T(8,128)(2,1)}, f32[128,1]{1,0:T(8,128)}) custom-call(bf16[128,4096]{1,0:T(8,128)(2,1)} %tokens_ref.3, f32[1,4096]{1,0:T(1,128)} %bitcast.43), custom_call_target="tpu_custom_call" | custom-call | tf_op jit(solution)/shard_map/pallas_call | solution.py:216
  67.7 6.0 %collective-permute-start.1 = (bf16[4096,128]{1,0:T(8,128)(2,1)}, bf16[4096,128]{1,0:T(8,128)(2,1)}, u32[]{:S(2)}, u32[]{:S(2)}) collective-permute-start(bf16[4096,128]{1,0:T(8,128)(2,1)} %get-tuple-element.9), channel_id=1, source_target_pairs={{0,1},{1,0},{2,3},{3,2},{4,5},{5,4},{6,7},{7,6},{8,9},{9,8},{10,11... | collective-permute-start | bytes 3145736 | tf_op jit(solution)/shard_map/ppermute | solution.py:142
  73.6 0.0 collective-permute-done.15.refs_14_
  73.7 6.7 %collective-permute-start = (f32[3584]{0:T(1024)}, f32[3584]{0:T(1024)}, u32[]{:S(2)}, u32[]{:S(2)}) collective-permute-start(f32[3584]{0:T(1024)} %param.8), channel_id=1, source_target_pairs={{0,2},{2,0},{1,3},{3,1},{4,6},{6,4},{5,7},{7,5},{8,10},{10,8},{9,1... | collective-permute-start | bytes 43016 | tf_op jit(solution)/shard_map/ppermute | solution.py:256
  80.4 0.1 reshape_reshape.6
  80.5 0.1 reshape_reshape.7
  80.6 0.8 slice.54
  81.4 0.0 collective-permute-done.14.refs_11_
  81.4 1.9 %collective-permute-start.16 = (bf16[48,32,128]{2,1,0:T(8,128)(2,1)}, bf16[48,32,128]{2,1,0:T(8,128)(2,1)S(1)}, u32[]{:S(2)}, u32[]{:S(2)}) collective-permute-start(bf16[48,32,128]{2,1,0:T(8,128)(2,1)} %slice.54), channel_id=1, source_target_pairs={{0,128},{1,5},{4,132},{5,9},{8,136},{9,13},{12,140},{13,1},{128,25... | collective-permute-start | bytes 1179656 | tf_op jit(solution)/shard_map/ppermute | solution.py:138
  83.3 0.8 slice.55
  84.1 0.0 collective-permute-done.10.refs_9_
  84.1 4.8 %collective-permute-start.17 = (bf16[48,32,128]{2,1,0:T(8,128)(2,1)}, bf16[48,32,128]{2,1,0:T(8,128)(2,1)S(1)}, u32[]{:S(2)}, u32[]{:S(2)}) collective-permute-start(bf16[48,32,128]{2,1,0:T(8,128)(2,1)} %slice.55), channel_id=1, source_target_pairs={{0,384},{1,13},{4,388},{5,1},{8,392},{9,5},{12,396},{13,9},{128,0}... | collective-permute-start | bytes 1179656 | tf_op jit(solution)/shard_map/ppermute | solution.py:138
  88.9 1.8 %slice.49 = bf16[48,32,128]{2,1,0:T(8,128)(2,1)} slice(bf16[96,32,128]{2,1,0:T(8,128)(2,1)} %collective-permute-done.10.refs_9_), slice={[0:48], [0:32], [0:128]} | slice | bytes 786432 | tf_op jit(solution)/shard_map/slice | solution.py:164
  90.6 0.0 collective-permute-done.9.refs_6_
  90.6 1.9 %collective-permute-start.11 = (bf16[48,32,128]{2,1,0:T(8,128)(2,1)}, bf16[48,32,128]{2,1,0:T(8,128)(2,1)S(1)}, u32[]{:S(2)}, u32[]{:S(2)}) collective-permute-start(bf16[48,32,128]{2,1,0:T(8,128)(2,1)} %slice.49), channel_id=1, source_target_pairs={{0,128},{1,5},{4,132},{5,9},{8,136},{9,13},{12,140},{13,1},{128,25... | collective-permute-start | bytes 1179656 | tf_op jit(solution)/shard_map/ppermute | solution.py:138
  92.5 1.8 %slice.50 = bf16[48,32,128]{2,1,0:T(8,128)(2,1)} slice(bf16[96,32,128]{2,1,0:T(8,128)(2,1)} %collective-permute-done.9.refs_6_), slice={[48:96], [0:32], [0:128]} | slice | bytes 786432 | tf_op jit(solution)/shard_map/slice | solution.py:165
  94.3 0.0 collective-permute-done
  94.3 4.6 %collective-permute-start.12 = (bf16[48,32,128]{2,1,0:T(8,128)(2,1)}, bf16[48,32,128]{2,1,0:T(8,128)(2,1)S(1)}, u32[]{:S(2)}, u32[]{:S(2)}) collective-permute-start(bf16[48,32,128]{2,1,0:T(8,128)(2,1)} %slice.50), channel_id=1, source_target_pairs={{0,384},{1,13},{4,388},{5,1},{8,392},{9,5},{12,396},{13,9},{128,0}... | collective-permute-start | bytes 1179656 | tf_op jit(solution)/shard_map/ppermute | solution.py:138
  98.9 0.1 copy.26
  99.0 0.7 reshape.43.refs_1_
  99.7 0.1 copy.25
  99.8 0.7 reshape.42.refs_0_
  100.5 0.7 broadcast_select_fusion.1
  101.2 0.1 stack.9
  101.3 0.1 stack.10
  101.4 1.0 copy.21
  102.3 0.0 collective-permute-done.1
  102.4 0.0 collective-permute-done.17.refs_13_
  102.4 0.0 collective-permute-done.11.refs_7_
  102.4 1.5 %collective-permute-done.12.refs_8_ = bf16[48,32,128]{2,1,0:T(8,128)(2,1)S(1)} collective-permute-done((bf16[48,32,128]{2,1,0:T(8,128)(2,1)}, bf16[48,32,128]{2,1,0:T(8,128)(2,1)S(1)}, u32[]{:S(2)}, u32[]{:S(2)}) %collective-permute-start.12) | collective-permute-done | bytes 393248 | tf_op jit(solution)/shard_map/ppermute | solution.py:138
  103.9 0.7 copy-done.8
  104.7 15.3 %shard_map.65 = (f32[64,64,128]{2,1,0:T(8,128)}, bf16[64,64,128]{2,1,0:T(8,128)(2,1)}) custom-call(s32[448]{0:T(512)} %reshape.42.refs_0_, s32[448]{0:T(512)} %reshape.43.refs_1_, f32[2,7,64,8]{3,2,1,0:T(8,128)} %bitcast.35, bf16[64,64,128]{2,1,0:T(8,128)(2,1)} %bitcast.37, bf16[64,64,128]{2,1,0:T(8,128)(2,1)} %bitcast.3.refs_4_, ...), custom_call_target="tpu_custom_call" | custom-call | tf_op jit(solution)/shard_map/pallas_call | solution.py:198
  120.0 3.7 %collective-permute-start.18 = (bf16[64,64,128]{2,1,0:T(8,128)(2,1)}, bf16[64,64,128]{2,1,0:T(8,128)(2,1)S(1)}, u32[]{:S(2)}, u32[]{:S(2)}) collective-permute-start(bf16[64,64,128]{2,1,0:T(8,128)(2,1)} %get-tuple-element.11), channel_id=1, source_target_pairs={{0,1},{1,0},{2,3},{3,2},{4,5},{5,4},{6,7},{7,6},{8,9},{9,8},{10,11... | collective-permute-start | bytes 3145736 | tf_op jit(solution)/shard_map/ppermute | solution.py:142
  123.7 2.5 %collective-permute-done.18 = bf16[64,64,128]{2,1,0:T(8,128)(2,1)S(1)} collective-permute-done((bf16[64,64,128]{2,1,0:T(8,128)(2,1)}, bf16[64,64,128]{2,1,0:T(8,128)(2,1)S(1)}, u32[]{:S(2)}, u32[]{:S(2)}) %collective-permute-start.18) | collective-permute-done | bytes 1048608 | tf_op jit(solution)/shard_map/ppermute | solution.py:142
  126.2 1.0 copy-done.4
  127.2 4.3 %shard_map.66 = bf16[128,4096]{1,0:T(8,128)(2,1)} custom-call(f32[4096,128]{1,0:T(8,128)} %bitcast.34, bf16[4096,128]{1,0:T(8,128)(2,1)} %bitcast.36, bf16[128,4096]{1,0:T(8,128)(2,1)} %tokens_ref.3, f32[1,4096]{1,0:T(1,128)} %bitcast.44, f32[128,1]{1,0:T(8,128)} %get-tuple-element.12.inverse_ref), custom_call_target="tpu_custom_call" | custom-call | tf_op jit(solution)/shard_map/pallas_call | solution.py:227
  (35 shorter events, 0.3 us)
Async XLA Ops:
  1.5 13.9 %collective-permute-start.3 = (bf16[2,1,3,32,128]{4,3,2,0,1:T(8,128)(2,1)S(1)}, bf16[2,1,3,32,128]{4,3,2,0,1:T(8,128)(2,1)S(1)}, u32[]{:S(2)}, u32[]{:S(2)}) collective-permute-start(bf16[2,1,3,32,128]{4,3,2,0,1:T(8,128)(2,1)S(1)} %broadcast_in_dim_reshape.3), channel_id=1, source_target_pairs={{0,16},{16,32},{32,48},{48,64},{64,80},{80,96},{96,112},{112,2},{2... | collective-permute-start | bytes 147464 | tf_op jit(solution)/shard_map/ppermute | solution.py:128
  5.9 13.8 %collective-permute-start.2 = (bf16[2,1,3,32,128]{4,3,2,0,1:T(8,128)(2,1)S(1)}, bf16[2,1,3,32,128]{4,3,2,0,1:T(8,128)(2,1)S(1)}, u32[]{:S(2)}, u32[]{:S(2)}) collective-permute-start(bf16[2,1,3,32,128]{4,3,2,0,1:T(8,128)(2,1)S(1)} %broadcast_in_dim_reshape.3), channel_id=1, source_target_pairs={{0,114},{16,0},{32,16},{48,32},{64,48},{80,64},{96,80},{112,96},{2... | collective-permute-start | bytes 147464 | tf_op jit(solution)/shard_map/ppermute | solution.py:128
  15.4 7.5 %collective-permute-start.4 = (bf16[2,2,3,32,128]{4,3,2,0,1:T(8,128)(2,1)S(1)}, bf16[2,2,3,32,128]{4,3,2,0,1:T(8,128)(2,1)S(1)}, u32[]{:S(2)}, u32[]{:S(2)}) collective-permute-start(bf16[2,2,3,32,128]{4,3,2,0,1:T(8,128)(2,1)S(1)} %pad_maximum_fusion.3), channel_id=1, source_target_pairs={{0,82},{16,98},{32,114},{48,0},{64,16},{80,32},{96,48},{112,64},{2... | collective-permute-start | bytes 294920 | tf_op jit(solution)/shard_map/ppermute | solution.py:128
  19.7 14.7 %collective-permute-start.5 = (bf16[2,3,3,32,128]{4,3,2,0,1:T(8,128)(2,1)S(1)}, bf16[2,3,3,32,128]{4,3,2,0,1:T(8,128)(2,1)S(1)}, u32[]{:S(2)}, u32[]{:S(2)}) collective-permute-start(bf16[2,3,3,32,128]{4,3,2,0,1:T(8,128)(2,1)S(1)} %pad_maximum_fusion.2), channel_id=1, source_target_pairs={{0,48},{16,64},{32,80},{48,96},{64,112},{80,2},{96,18},{112,34},{2... | collective-permute-start | bytes 442376 | tf_op jit(solution)/shard_map/ppermute | solution.py:128
  34.5 9.3 %collective-permute-start.6 = (bf16[2,24,32,128]{3,2,1,0:T(8,128)(2,1)S(1)}, bf16[2,24,32,128]{3,2,1,0:T(8,128)(2,1)S(1)}, u32[]{:S(2)}, u32[]{:S(2)}) collective-permute-start(bf16[2,24,32,128]{3,2,1,0:T(8,128)(2,1)S(1)} %bitcast.40), channel_id=1, source_target_pairs={{0,12},{1,385},{4,0},{5,389},{8,4},{9,393},{12,8},{13,397},{128,14... | collective-permute-start | bytes 1179656 | tf_op jit(solution)/shard_map/ppermute | solution.py:138
  39.1 10.0 %collective-permute-start.7 = (bf16[2,24,32,128]{3,2,1,0:T(8,128)(2,1)S(1)}, bf16[2,24,32,128]{3,2,1,0:T(8,128)(2,1)S(1)}, u32[]{:S(2)}, u32[]{:S(2)}) collective-permute-start(bf16[2,24,32,128]{3,2,1,0:T(8,128)(2,1)S(1)} %bitcast.41), channel_id=1, source_target_pairs={{0,4},{1,129},{4,8},{5,133},{8,12},{9,137},{12,0},{13,141},{128,13... | collective-permute-start | bytes 1179656 | tf_op jit(solution)/shard_map/ppermute | solution.py:138
  43.8 7.6 %collective-permute-start.13 = (bf16[24,32,128]{2,1,0:T(8,128)(2,1)S(1)}, bf16[24,32,128]{2,1,0:T(8,128)(2,1)S(1)}, u32[]{:S(2)}, u32[]{:S(2)}) collective-permute-start(bf16[24,32,128]{2,1,0:T(8,128)(2,1)S(1)} %get-tuple-element.15), channel_id=1, source_target_pairs={{0,12},{1,385},{4,0},{5,389},{8,4},{9,393},{12,8},{13,397},{128,14... | collective-permute-start | bytes 589832 | tf_op jit(solution)/shard_map/ppermute | solution.py:138
  49.2 9.0 %collective-permute-start.8 = (bf16[24,32,128]{2,1,0:T(8,128)(2,1)S(1)}, bf16[24,32,128]{2,1,0:T(8,128)(2,1)S(1)}, u32[]{:S(2)}, u32[]{:S(2)}) collective-permute-start(bf16[24,32,128]{2,1,0:T(8,128)(2,1)S(1)} %get-tuple-element.18), channel_id=1, source_target_pairs={{0,4},{1,129},{4,8},{5,133},{8,12},{9,137},{12,0},{13,141},{128,13... | collective-permute-start | bytes 589832 | tf_op jit(solution)/shard_map/ppermute | solution.py:138
  51.5 28.9 %copy-start.10 = (s32[224,4]{0,1:T(4,128)S(1)}, s32[224,4]{0,1:T(4,128)}, u32[]{:S(2)}) copy-start(s32[224,4]{0,1:T(4,128)} %param.11) | copy-start | bytes 10756
  51.5 29.1 %copy-start.9 = (s32[224,4]{0,1:T(4,128)S(1)}, s32[224,4]{0,1:T(4,128)}, u32[]{:S(2)}) copy-start(s32[224,4]{0,1:T(4,128)} %param.10) | copy-start | bytes 10756
  51.6 32.5 %copy-start = (bf16[96,32,128]{2,1,0:T(8,128)(2,1)}, bf16[96,32,128]{2,1,0:T(8,128)(2,1)S(1)}, u32[]{:S(2)}) copy-start(bf16[96,32,128]{2,1,0:T(8,128)(2,1)S(1)} %pad_maximum_fusion.1.refs_10_) | copy-start | bytes 2359300
  51.6 22.1 %collective-permute-start.15 = (bf16[96,32,128]{2,1,0:T(8,128)(2,1)S(1)}, bf16[96,32,128]{2,1,0:T(8,128)(2,1)S(1)}, u32[]{:S(2)}, u32[]{:S(2)}) collective-permute-start(bf16[96,32,128]{2,1,0:T(8,128)(2,1)S(1)} %pad_maximum_fusion.1.refs_10_), channel_id=1, source_target_pairs={{0,128},{1,5},{4,132},{5,9},{8,136},{9,13},{12,140},{13,1},{128,25... | collective-permute-start | bytes 2359304 | tf_op jit(solution)/shard_map/ppermute | solution.py:138
  54.7 26.7 %collective-permute-start.14 = (bf16[96,32,128]{2,1,0:T(8,128)(2,1)S(1)}, bf16[96,32,128]{2,1,0:T(8,128)(2,1)S(1)}, u32[]{:S(2)}, u32[]{:S(2)}) collective-permute-start(bf16[96,32,128]{2,1,0:T(8,128)(2,1)S(1)} %pad_maximum_fusion.1.refs_10_), channel_id=1, source_target_pairs={{0,384},{1,13},{4,388},{5,1},{8,392},{9,5},{12,396},{13,9},{128,0}... | collective-permute-start | bytes 2359304 | tf_op jit(solution)/shard_map/ppermute | solution.py:138
  58.3 36.0 %copy-start.1 = (bf16[96,32,128]{2,1,0:T(8,128)(2,1)}, bf16[96,32,128]{2,1,0:T(8,128)(2,1)S(1)}, u32[]{:S(2)}) copy-start(bf16[96,32,128]{2,1,0:T(8,128)(2,1)S(1)} %pad_maximum_fusion.refs_5_) | copy-start | bytes 2359300
  58.3 25.7 %collective-permute-start.10 = (bf16[96,32,128]{2,1,0:T(8,128)(2,1)S(1)}, bf16[96,32,128]{2,1,0:T(8,128)(2,1)}, u32[]{:S(2)}, u32[]{:S(2)}) collective-permute-start(bf16[96,32,128]{2,1,0:T(8,128)(2,1)S(1)} %pad_maximum_fusion.refs_5_), channel_id=1, source_target_pairs={{0,128},{1,5},{4,132},{5,9},{8,136},{9,13},{12,140},{13,1},{128,25... | collective-permute-start | bytes 2359304 | tf_op jit(solution)/shard_map/ppermute | solution.py:138
  60.3 30.4 %collective-permute-start.9 = (bf16[96,32,128]{2,1,0:T(8,128)(2,1)S(1)}, bf16[96,32,128]{2,1,0:T(8,128)(2,1)}, u32[]{:S(2)}, u32[]{:S(2)}) collective-permute-start(bf16[96,32,128]{2,1,0:T(8,128)(2,1)S(1)} %pad_maximum_fusion.refs_5_), channel_id=1, source_target_pairs={{0,384},{1,13},{4,388},{5,1},{8,392},{9,5},{12,396},{13,9},{128,0}... | collective-permute-start | bytes 2359304 | tf_op jit(solution)/shard_map/ppermute | solution.py:138
  67.7 34.7 %collective-permute-start.1 = (bf16[4096,128]{1,0:T(8,128)(2,1)}, bf16[4096,128]{1,0:T(8,128)(2,1)}, u32[]{:S(2)}, u32[]{:S(2)}) collective-permute-start(bf16[4096,128]{1,0:T(8,128)(2,1)} %get-tuple-element.9), channel_id=1, source_target_pairs={{0,1},{1,0},{2,3},{3,2},{4,5},{5,4},{6,7},{7,6},{8,9},{9,8},{10,11... | collective-permute-start | bytes 3145736 | tf_op jit(solution)/shard_map/ppermute | solution.py:142
  73.7 28.7 %copy-start.2 = (bf16[96,32,128]{2,1,0:T(8,128)(2,1)}, bf16[96,32,128]{2,1,0:T(8,128)(2,1)S(1)}, u32[]{:S(2)}) copy-start(bf16[96,32,128]{2,1,0:T(8,128)(2,1)S(1)} %collective-permute-done.15.refs_14_) | copy-start | bytes 2359300
  73.7 20.7 %collective-permute-start = (f32[3584]{0:T(1024)}, f32[3584]{0:T(1024)}, u32[]{:S(2)}, u32[]{:S(2)}) collective-permute-start(f32[3584]{0:T(1024)} %param.8), channel_id=1, source_target_pairs={{0,2},{2,0},{1,3},{3,1},{4,6},{6,4},{5,7},{7,5},{8,10},{10,8},{9,1... | collective-permute-start | bytes 43016 | tf_op jit(solution)/shard_map/ppermute | solution.py:256
  81.4 22.5 %copy-start.3 = (bf16[96,32,128]{2,1,0:T(8,128)(2,1)}, bf16[96,32,128]{2,1,0:T(8,128)(2,1)S(1)}, u32[]{:S(2)}) copy-start(bf16[96,32,128]{2,1,0:T(8,128)(2,1)S(1)} %collective-permute-done.14.refs_11_) | copy-start | bytes 2359300
  81.4 21.0 %collective-permute-start.16 = (bf16[48,32,128]{2,1,0:T(8,128)(2,1)}, bf16[48,32,128]{2,1,0:T(8,128)(2,1)S(1)}, u32[]{:S(2)}, u32[]{:S(2)}) collective-permute-start(bf16[48,32,128]{2,1,0:T(8,128)(2,1)} %slice.54), channel_id=1, source_target_pairs={{0,128},{1,5},{4,132},{5,9},{8,136},{9,13},{12,140},{13,1},{128,25... | collective-permute-start | bytes 1179656 | tf_op jit(solution)/shard_map/ppermute | solution.py:138
  84.1 18.3 %collective-permute-start.17 = (bf16[48,32,128]{2,1,0:T(8,128)(2,1)}, bf16[48,32,128]{2,1,0:T(8,128)(2,1)S(1)}, u32[]{:S(2)}, u32[]{:S(2)}) collective-permute-start(bf16[48,32,128]{2,1,0:T(8,128)(2,1)} %slice.55), channel_id=1, source_target_pairs={{0,384},{1,13},{4,388},{5,1},{8,392},{9,5},{12,396},{13,9},{128,0}... | collective-permute-start | bytes 1179656 | tf_op jit(solution)/shard_map/ppermute | solution.py:138
  90.6 11.8 %collective-permute-start.11 = (bf16[48,32,128]{2,1,0:T(8,128)(2,1)}, bf16[48,32,128]{2,1,0:T(8,128)(2,1)S(1)}, u32[]{:S(2)}, u32[]{:S(2)}) collective-permute-start(bf16[48,32,128]{2,1,0:T(8,128)(2,1)} %slice.49), channel_id=1, source_target_pairs={{0,128},{1,5},{4,132},{5,9},{8,136},{9,13},{12,140},{13,1},{128,25... | collective-permute-start | bytes 1179656 | tf_op jit(solution)/shard_map/ppermute | solution.py:138
  94.3 9.6 %collective-permute-start.12 = (bf16[48,32,128]{2,1,0:T(8,128)(2,1)}, bf16[48,32,128]{2,1,0:T(8,128)(2,1)S(1)}, u32[]{:S(2)}, u32[]{:S(2)}) collective-permute-start(bf16[48,32,128]{2,1,0:T(8,128)(2,1)} %slice.50), channel_id=1, source_target_pairs={{0,384},{1,13},{4,388},{5,1},{8,392},{9,5},{12,396},{13,9},{128,0}... | collective-permute-start | bytes 1179656 | tf_op jit(solution)/shard_map/ppermute | solution.py:138
  102.3 1.6 %copy-start.5 = (bf16[48,32,128]{2,1,0:T(8,128)(2,1)}, bf16[48,32,128]{2,1,0:T(8,128)(2,1)S(1)}, u32[]{:S(2)}) copy-start(bf16[48,32,128]{2,1,0:T(8,128)(2,1)S(1)} %collective-permute-done.16.refs_12_) | copy-start | bytes 1179652
  102.4 1.6 %copy-start.6 = (bf16[48,32,128]{2,1,0:T(8,128)(2,1)}, bf16[48,32,128]{2,1,0:T(8,128)(2,1)S(1)}, u32[]{:S(2)}) copy-start(bf16[48,32,128]{2,1,0:T(8,128)(2,1)S(1)} %collective-permute-done.17.refs_13_) | copy-start | bytes 1179652
  102.4 1.5 %copy-start.7 = (bf16[48,32,128]{2,1,0:T(8,128)(2,1)}, bf16[48,32,128]{2,1,0:T(8,128)(2,1)S(1)}, u32[]{:S(2)}) copy-start(bf16[48,32,128]{2,1,0:T(8,128)(2,1)S(1)} %collective-permute-done.11.refs_7_) | copy-start | bytes 1179652
  103.9 0.8 copy-start.8
  120.0 6.2 %collective-permute-start.18 = (bf16[64,64,128]{2,1,0:T(8,128)(2,1)}, bf16[64,64,128]{2,1,0:T(8,128)(2,1)S(1)}, u32[]{:S(2)}, u32[]{:S(2)}) collective-permute-start(bf16[64,64,128]{2,1,0:T(8,128)(2,1)} %get-tuple-element.11), channel_id=1, source_target_pairs={{0,1},{1,0},{2,3},{3,2},{4,5},{5,4},{6,7},{7,6},{8,9},{9,8},{10,11... | collective-permute-start | bytes 3145736 | tf_op jit(solution)/shard_map/ppermute | solution.py:142
  126.2 1.0 copy-start.4

commit v2 on v1

v2 whole, which is shorter than its diff:
```python
import jax
import jax.numpy as jnp
from jax import lax
from jax.experimental import pallas as pl
from jax.experimental.pallas import tpu as pltpu
from jax.sharding import Mesh
from jax.sharding import PartitionSpec as P

BLOCK = 64
HALF = BLOCK // 2
EPS = 1e-05
LANES = 128
GROUP = 8
NX, NY, NZ = 4, 4, 8
SIDE = 4
AXES = ("y", "zl", "x", "zh", "core")
SMEM = pl.BlockSpec(memory_space=pltpu.SMEM)
VMEM = pl.BlockSpec(memory_space=pltpu.VMEM)


def on_chip(x):
    return pltpu.with_memory_space_constraint(x, pltpu.VMEM)


def norm_kernel(tokens_ref, gain_ref, feat_ref, inverse_ref):
    x = tokens_ref[...].astype(jnp.float32)
    inverse = 1.0 / jnp.sqrt(jnp.mean(x * x, axis=1, keepdims=True) + EPS)
    inverse_ref[...] = inverse
    scaled = ((x * inverse) * gain_ref[...]).astype(jnp.bfloat16)
    for at in range(0, x.shape[1], LANES):
        feat_ref[at : at + LANES, :] = scaled[:, at : at + LANES].T


def sparse_kernel(columns, per_column, tile_ref, row_ref, unit_ref, mine_ref, other_ref, *refs):
    parts, (keep_ref, send_ref, away_ref, w_ref, sems) = refs[:8], refs[8:]
    count = mine_ref.shape[2]
    size = parts[0].shape[0]
    copies = []
    for i, source in enumerate(parts):
        run, at = i // SIDE, i % SIDE
        target = w_ref.at[run, pl.ds(at * size, size)]
        copies.append(pltpu.make_async_copy(source, target, sems.at[run, at]))
    for copy in copies:
        copy.start()
    keep_ref[...] = jnp.zeros_like(keep_ref)
    away_ref[...] = jnp.zeros_like(away_ref)
    blank = jnp.zeros((BLOCK, 2 * count), jnp.bfloat16)

    def work(run):
        def group(g, carry):
            first = (run * columns + g * GROUP) * per_column
            units = unit_ref[run, g]

            def forward(j):
                at = first + j * per_column
                rows = [row_ref[at + k] for k in range(per_column)]
                stack = jnp.concatenate(
                    [w_ref[run, tile_ref[at + k]] for k in range(per_column)], axis=0
                )
                turned = stack.T
                lhs = jnp.concatenate([turned[:BLOCK], turned[BLOCK:]], axis=1)
                mine = [mine_ref[r] for r in rows]
                other = [other_ref[r] for r in rows]
                rhs = jnp.concatenate(
                    [
                        jnp.concatenate([p[:HALF] for p in side] + [p[HALF:] for p in side], axis=0)
                        for side in (mine, other)
                    ],
                    axis=1,
                )
                preact = jnp.dot(lhs, rhs, preferred_element_type=jnp.float32)
                gating = jax.nn.sigmoid(preact)
                grad_act = units[:, j : j + 1] * (preact * gating)
                grad_pre = grad_act * (gating * (1.0 + preact * (1.0 - gating)))
                return rows, stack, grad_pre.astype(jnp.bfloat16)

            def backward(rows, stack, grad_pre):
                upper = jnp.dot(
                    stack,
                    jnp.concatenate([grad_pre, blank], axis=0),
                    preferred_element_type=jnp.float32,
                )
                lower = jnp.dot(
                    stack,
                    jnp.concatenate([blank, grad_pre], axis=0),
                    preferred_element_type=jnp.float32,
                )
                for ref, lanes in ((keep_ref, slice(0, count)), (away_ref, slice(count, None))):
                    sums = []
                    for k in range(per_column):
                        span = slice(k * HALF, (k + 1) * HALF)
                        term = jnp.concatenate([upper[span, lanes], lower[span, lanes]], axis=0)
                        sums.append(ref[rows[k]] + term)
                    for k in range(per_column):
                        ref[rows[k]] = sums[k]

            held = [forward(j) for j in range(GROUP)]
            for piece in held:
                backward(*piece)
            return carry

        lax.fori_loop(0, columns // GROUP, group, 0)

    for run in range(2):
        for copy in copies[4 * run : 4 * run + 4]:
            copy.wait()
        work(run)
    send_ref[...] = away_ref[...].astype(jnp.bfloat16)


def close_kernel(keep_ref, came_ref, tokens_ref, gain_ref, inverse_ref, out_ref, grad_ref):
    inverse = inverse_ref[...]
    width = tokens_ref.shape[1]
    total = jnp.zeros((tokens_ref.shape[0], LANES), jnp.float32)
    for at in range(0, width, LANES):
        span = slice(at, at + LANES)
        grad = (keep_ref[span, :] + came_ref[span, :].astype(jnp.float32)).T
        grad = grad * gain_ref[:, span]
        grad_ref[:, span] = grad
        total += grad * (tokens_ref[:, span].astype(jnp.float32) * inverse)
    mixing = jnp.sum(total, axis=1, keepdims=True) * (1.0 / width)
    for at in range(0, width, LANES):
        span = slice(at, at + LANES)
        normed = tokens_ref[:, span].astype(jnp.float32) * inverse
        out_ref[:, span] = ((grad_ref[:, span] - normed * mixing) * inverse).astype(jnp.bfloat16)


def along_z(v, step):
    size = 2 * NZ
    pairs = []
    for z in range(size):
        for core in range(2):
            to = (z + (step if core == 0 else -step)) % size
            pairs.append([((at % NZ) * 2 + at // NZ) * 2 + core for at in (z, to)])
    return lax.ppermute(v, ("zl", "zh", "core"), pairs)


def along_side(v, step, leg):
    pairs = []
    for y in range(NY):
        for x in range(NX):
            for core in range(2):
                to_y, to_x = (y, (x + step) % NX) if core == leg else ((y + step) % NY, x)
                pairs.append(((y * NX + x) * 2 + core, (to_y * NX + to_x) * 2 + core))
    return lax.ppermute(v, ("y", "x", "core"), pairs)


def swap_cores(v):
    return lax.ppermute(v, "core", [(0, 1), (1, 0)])


def join_kernel(line_ref, ahead_ref, across_ref, back_ref, *plane_refs):
    size = line_ref.shape[1]
    for run, plane_ref in enumerate(plane_refs):
        for i, ref in enumerate((line_ref, ahead_ref, across_ref, back_ref)):
            plane_ref[i * size : (i + 1) * size] = ref[run]


def join(*parts):
    runs, size, *tile = parts[0].shape
    return pl.pallas_call(
        join_kernel,
        out_shape=[pltpu.VMEM((SIDE * size, *tile), parts[0].dtype)] * runs,
        in_specs=[VMEM] * len(parts),
        out_specs=[VMEM] * runs,
        compiler_params=pltpu.CompilerParams(vmem_limit_bytes=1 << 20),
    )(*map(on_chip, parts))


def of_core(table, core):
    paired = table.reshape(*table.shape[:-4], 2, 2, *table.shape[-3:])
    return lax.dynamic_index_in_dim(paired, core, paired.ndim - 4, keepdims=False)


def gather_tiles(own, core, early):
    _, slots = own.shape[:2]
    mine = of_core(own, core)
    far = along_z(own, 3)
    opposite = along_z(mine, 4)
    middle = along_z(own, 2)
    near = along_z(own, 1)
    near, middle, far, early = lax.optimization_barrier((near, middle, far, early))
    side = jnp.stack([near, middle, far])
    theirs = swap_cores(of_core(side, 1 - core))
    line = jnp.concatenate([mine[None], of_core(side, core), opposite[None], theirs], axis=0)
    line = line.transpose(1, 0, 2, 3, 4).reshape(2, NZ * slots, HALF, 2 * BLOCK)
    across, back, ahead = along_side(line, 2, 0), along_side(line, 1, 0), along_side(line, -1, 0)
    planes = join(line, ahead, across, back)
    back_0, ahead_1 = along_side(planes[0], 1, 1), along_side(planes[1], -1, 1)
    back_1, ahead_0 = along_side(planes[1], 1, 1), along_side(planes[0], -1, 1)
    across_0, across_1 = along_side(back_0, 1, 1), along_side(ahead_1, -1, 1)
    pieces = [planes[0], ahead_0, across_0, back_0, planes[1], ahead_1, across_1, back_1]
    return pieces, early


def tile_places(block_slot, slots, y, zl, x, core):
    owner, place = block_slot // slots, block_slot % slots
    step_x = (owner % NX - x) % NX
    step_z = ((owner // NX) % NZ - zl) * (2 * core - 1) % NZ
    step_z = jnp.where(step_z > NZ // 2, 3 * NZ // 2 - step_z, step_z)
    step_y = (owner // (NX * NZ) - y) % NY
    first = jnp.where(core == 0, step_x, step_y)
    second = jnp.where(core == 0, step_y, step_x)
    return ((second * SIDE + first) * NZ + step_z) * slots + place


def sparse_call(columns, per_column, places, rows, units, mine, other, tiles):
    row_blocks, _, count = mine.shape

    def body(*refs):
        sparse_kernel(columns, per_column, *refs)

    return pl.pallas_call(
        body,
        out_shape=(
            pltpu.VMEM((row_blocks, BLOCK, count), jnp.float32),
            pltpu.VMEM((row_blocks, BLOCK, count), jnp.bfloat16),
        ),
        in_specs=[SMEM, SMEM] + [VMEM] * 11,
        out_specs=(VMEM, VMEM),
        scratch_shapes=[
            pltpu.VMEM((row_blocks, BLOCK, count), jnp.float32),
            pltpu.VMEM((2, SIDE * tiles[0].shape[0], HALF, 2 * BLOCK), jnp.bfloat16),
            pltpu.SemaphoreType.DMA((2, 4)),
        ],
        compiler_params=pltpu.CompilerParams(vmem_limit_bytes=14 << 20),
    )(
        places, rows, on_chip(units), on_chip(mine), on_chip(other),
        *map(on_chip, tiles),
    )


def norm_call(tokens, gain):
    count, width = tokens.shape
    return pl.pallas_call(
        norm_kernel,
        out_shape=(
            pltpu.VMEM((width, count), jnp.bfloat16),
            pltpu.VMEM((count, 1), jnp.float32),
        ),
        in_specs=[VMEM, VMEM],
        out_specs=(VMEM, VMEM),
        compiler_params=pltpu.CompilerParams(vmem_limit_bytes=6 << 20),
    )(on_chip(tokens), gain)


def close_call(keep, came, tokens, gain, inverse):
    count, width = tokens.shape
    return pl.pallas_call(
        close_kernel,
        out_shape=jax.ShapeDtypeStruct((count, width), jnp.bfloat16),
        in_specs=[VMEM] * 5,
        out_specs=VMEM,
        scratch_shapes=[pltpu.VMEM((count, width), jnp.float32)],
        compiler_params=pltpu.CompilerParams(vmem_limit_bytes=6 << 20),
    )(
        on_chip(keep.reshape(width, count)), on_chip(came.reshape(width, count)), on_chip(tokens),
        gain, on_chip(inverse),
    )


def unit_kernel(high_ref, near_ref, far_ref, units_ref):
    near, far, high = near_ref[...], far_ref[...], high_ref[0]
    groups = near.shape[0] // GROUP
    for run in range(2):
        turned = jnp.where(high == run, near, far).T
        for g in range(groups):
            units_ref[run, g] = turned[:, g * GROUP : (g + 1) * GROUP]


def unit_call(high, near, far):
    columns, block = near.shape
    return pl.pallas_call(
        unit_kernel,
        out_shape=pltpu.VMEM((2, columns // GROUP, block, GROUP), jnp.float32),
        in_specs=[SMEM, VMEM, VMEM],
        out_specs=VMEM,
        compiler_params=pltpu.CompilerParams(vmem_limit_bytes=1 << 20),
    )(high, on_chip(near), on_chip(far))


def pack_tiles(tiles):
    lead = tiles.shape[:-1]
    split = tiles.reshape(*lead, 2, HALF, BLOCK)
    return jnp.moveaxis(split, -3, -2).reshape(*lead, HALF, 2 * BLOCK)


def on_device(tokens, norm_gain, penalty, weight_tiles, block_rows, block_slot):
    y, zl, x, zh, core = (lax.axis_index(name) for name in AXES)
    runs, slots, _ = weight_tiles.shape
    count, width = tokens.shape
    columns, per_column = block_rows.shape[0] // runs, block_rows.shape[1]

    def of_runs(table):
        paired = table.reshape(2, 2, columns * per_column)
        return lax.dynamic_index_in_dim(paired, core, 1, keepdims=False).reshape(-1)

    rows = of_runs(block_rows)
    places = of_runs(tile_places(block_slot, slots, y, zl, x, core))
    near = penalty.reshape(columns, BLOCK)
    own = pack_tiles(weight_tiles)
    tiles, (rows, places, near, high) = gather_tiles(own, core, (rows, places, near, zh.reshape(1)))
    gain = norm_gain.reshape(1, width)
    features, inverse = norm_call(tokens, gain)
    other = swap_cores(features)
    distant = lax.ppermute(near, "zh", [(0, 1), (1, 0)])
    units = unit_call(high, near, distant)
    blocks = (width // BLOCK, BLOCK, count)
    keep, send = sparse_call(
        columns, per_column, places, rows, units, features.reshape(blocks), other.reshape(blocks), tiles
    )
    came = swap_cores(send)
    return close_call(keep, came, tokens, gain, inverse)


def solution(mesh):
    fine = Mesh(mesh.devices.reshape(NY, NZ, NX, 2, 2), AXES)
    placed = (P(AXES, None), P(), P(("zh", "core")), P(None, ("y", "zl", "x"), None), P(), P())

    return jax.shard_map(
        on_device, mesh=fine, in_specs=placed, out_specs=P(AXES, None), check_vma=False
    )
```

time: 133 us -> 122 us (0.917)
  Pallas kernels: 22.5 us -> 14.8 us
  local copies, waits for them, and re-layouts: 11.3 us -> 3.76 us
  waiting for transfers between devices: 19.2 us -> 24.6 us
    ppermute x12 -> x9, waiting for transfers between devices: 4.91 us -> 17.9 us  [along_side(): return lax.ppermute(v, ('y', 'x', 'core'), pairs)]
    ppermute x12 -> x9, starting transfers between devices: 39.7 us -> 32 us  [along_side(): return lax.ppermute(v, ('y', 'x', 'core'), pairs)]
    ppermute x5, waiting for transfers between devices: 11.8 us -> 4.43 us  [the longest x4 3.67 us: along_z(): return lax.ppermute(v, ('zl', 'zh', 'core'), pairs)]
    pallas_call x2 -> x4, Pallas kernels: 18.1 us -> 12.6 us  [the longest x1 11.6 us: sparse_call(): pl.pallas_call(body, out_shape=(pltpu.VMEM((row_blocks, BLOCK, count), jn...]
    ppermute x5, starting transfers between devices: 27.6 us -> 33.2 us  [the longest x4 24.8 us: along_z(): return lax.ppermute(v, ('zl', 'zh', 'core'), pairs)]
    slice x5 -> x0, local copies, waits for them, and re-layouts: 5.14 us -> none  [the longest x2 2.56 us: gather_tiles(): from_ahead = along_side(ahead[half:], -1, 1)]
    pallas_call x1, Pallas kernels: 4.34 us -> 2.27 us  [close_call(): pl.pallas_call(close_kernel, out_shape=jax.ShapeDtypeStruct((count, width...]
    ppermute x2 -> x3, starting transfers between devices: 9.65 us -> 11.2 us  [swap_cores(): return lax.ppermute(v, 'core', [(0, 1), (1, 0)])]
  transfers between devices with their start and end apart: 19 -> 17, of which waited for: 7 -> 7; matrix products, arithmetic and copies ran while one was open for 7% -> 3% of each run, Pallas kernels for 2% -> 1%
where the time goes in v2:
time: 122 us; the launch traced here: 121 us
  starting transfers between devices  76.5 us (63%)
  waiting for transfers between devices  24.6 us (20%)
  Pallas kernels  14.8 us (12%)
  local copies, waits for them, and re-layouts  3.76 us (3%)
    ppermute x9, starting transfers between devices, along_side(): return lax.ppermute(v, ('y', 'x', 'core'), pairs)  32 us
    ppermute x4, starting transfers between devices, along_z(): return lax.ppermute(v, ('zl', 'zh', 'core'), pairs)  24.8 us
    ppermute x9, waiting for transfers between devices, along_side(): return lax.ppermute(v, ('y', 'x', 'core'), pairs)  17.9 us
    pallas_call x1, Pallas kernels, sparse_call(): pl.pallas_call(body, out_shape=(pltpu.VMEM((row_blocks, BLOCK, count), jn...  11.6 us
    ppermute x3, starting transfers between devices, swap_cores(): return lax.ppermute(v, 'core', [(0, 1), (1, 0)])  11.2 us
    ppermute x1, starting transfers between devices, on_device(): distant = lax.ppermute(near, 'zh', [(0, 1), (1, 0)])  8.36 us
    ppermute x4, waiting for transfers between devices, along_z(): return lax.ppermute(v, ('zl', 'zh', 'core'), pairs)  3.67 us
  transfers between devices with their start and end apart: 17, of which 7 were waited for; matrix products, arithmetic and copies ran while one was open for 3% of the time, Pallas kernels for 1%

profile of v2, /device:TPU:1, one launch (start us, length us, event | category | flops | bytes accessed | tf_op | source)
XLA Modules:
  0.0 120.8 jit_solution(15301713702693250489)
XLA Ops:
  0.0 1.1 reshape.53
  1.1 0.2 copy.15
  1.3 0.1 reshape.54
  1.4 12.8 %collective-permute-start.2 = (bf16[4,3,32,128]{3,2,1,0:T(8,128)(2,1)S(1)}, bf16[4,3,32,128]{3,2,1,0:T(8,128)(2,1)S(1)}, u32[]{:S(2)}, u32[]{:S(2)}) collective-permute-start(bf16[4,3,32,128]{3,2,1,0:T(8,128)(2,1)S(1)} %reshape.54), channel_id=1, source_target_pairs={{0,48},{1,83},{16,64},{17,99},{32,80},{33,115},{48,96},{49,1},{64,... | collective-permute-start | bytes 294920 | tf_op jit(solution)/shard_map/ppermute | solution.py:135
  14.3 4.3 %collective-permute-start.1 = (bf16[4,3,32,128]{3,2,1,0:T(8,128)(2,1)S(1)}, bf16[4,3,32,128]{3,2,1,0:T(8,128)(2,1)S(1)}, u32[]{:S(2)}, u32[]{:S(2)}) collective-permute-start(bf16[4,3,32,128]{3,2,1,0:T(8,128)(2,1)S(1)} %reshape.54), channel_id=1, source_target_pairs={{0,32},{1,99},{16,48},{17,115},{32,64},{33,1},{48,80},{49,17},{64,... | collective-permute-start | bytes 294920 | tf_op jit(solution)/shard_map/ppermute | solution.py:135
  18.6 2.6 %collective-permute-start = (bf16[4,3,32,128]{3,2,1,0:T(8,128)(2,1)S(1)}, bf16[4,3,32,128]{3,2,1,0:T(8,128)(2,1)S(1)}, u32[]{:S(2)}, u32[]{:S(2)}) collective-permute-start(bf16[4,3,32,128]{3,2,1,0:T(8,128)(2,1)S(1)} %reshape.54), channel_id=1, source_target_pairs={{0,16},{1,115},{16,32},{17,1},{32,48},{33,17},{48,64},{49,33},{64,... | collective-permute-start | bytes 294920 | tf_op jit(solution)/shard_map/ppermute | solution.py:135
  21.2 0.7 fusion.9
  22.0 0.1 reshape_reshape.3
  22.1 0.8 reshape.59.near_ref
  22.9 0.1 copy.12
  23.0 0.1 reshape.57
  23.1 0.8 copy.11
  23.9 0.1 reshape.55
  24.1 0.1 reshape.58.refs_0_
  24.2 0.1 reshape.56.refs_1_
  24.3 0.0 collective-permute-done.2
  24.3 0.0 collective-permute-done.1
  24.3 0.0 collective-permute-done
  24.3 0.0 copy-start
  24.3 0.0 copy-start.1
  24.4 2.1 %collective-permute-start.6 = (bf16[3,2,3,32,128]{4,3,2,1,0:T(8,128)(2,1)S(1)}, bf16[3,2,3,32,128]{4,3,2,1,0:T(8,128)(2,1)S(1)}, u32[]{:S(2)}, u32[]{:S(2)}) collective-permute-start(bf16[3,2,3,32,128]{4,3,2,1,0:T(8,128)(2,1)S(1)} %get-tuple-element.32), channel_id=1, source_target_pairs={{0,1},{1,0},{2,3},{3,2},{4,5},{5,4},{6,7},{7,6},{8,9},{9,8},{10,11... | collective-permute-start | bytes 442376 | tf_op jit(solution)/shard_map/ppermute | solution.py:149
  26.5 5.1 %collective-permute-start.5 = (bf16[2,3,32,128]{3,2,1,0:T(8,128)(2,1)S(1)}, bf16[2,3,32,128]{3,2,1,0:T(8,128)(2,1)S(1)}, u32[]{:S(2)}, u32[]{:S(2)}) collective-permute-start(bf16[2,3,32,128]{3,2,1,0:T(8,128)(2,1)S(1)} %get-tuple-element.34), channel_id=1, source_target_pairs={{0,64},{1,67},{16,80},{17,83},{32,96},{33,99},{48,112},{49,115},{6... | collective-permute-start | bytes 147464 | tf_op jit(solution)/shard_map/ppermute | solution.py:135
  31.6 3.7 %collective-permute-done.5 = bf16[2,3,32,128]{3,2,1,0:T(8,128)(2,1)S(1)} collective-permute-done((bf16[2,3,32,128]{3,2,1,0:T(8,128)(2,1)S(1)}, bf16[2,3,32,128]{3,2,1,0:T(8,128)(2,1)S(1)}, u32[]{:S(2)}, u32[]{:S(2)}) %collective-permute-start.5) | collective-permute-done | bytes 49184 | tf_op jit(solution)/shard_map/ppermute | solution.py:135
  35.2 0.0 collective-permute-done.6
  35.2 0.1 maximum_bitcast_fusion
  35.3 3.2 %collective-permute-start.9 = (bf16[2,24,32,128]{3,2,1,0:T(8,128)(2,1)S(1)}, bf16[2,24,32,128]{3,2,1,0:T(8,128)(2,1)S(1)}, u32[]{:S(2)}, u32[]{:S(2)}) collective-permute-start(bf16[2,24,32,128]{3,2,1,0:T(8,128)(2,1)S(1)} %bitcast.27), channel_id=1, source_target_pairs={{0,4},{1,129},{4,8},{5,133},{8,12},{9,137},{12,0},{13,141},{128,13... | collective-permute-start | bytes 1179656 | tf_op jit(solution)/shard_map/ppermute | solution.py:145
  38.5 4.5 %collective-permute-start.8 = (bf16[2,24,32,128]{3,2,1,0:T(8,128)(2,1)S(1)}, bf16[2,24,32,128]{3,2,1,0:T(8,128)(2,1)S(1)}, u32[]{:S(2)}, u32[]{:S(2)}) collective-permute-start(bf16[2,24,32,128]{3,2,1,0:T(8,128)(2,1)S(1)} %bitcast.28), channel_id=1, source_target_pairs={{0,8},{1,257},{4,12},{5,261},{8,0},{9,265},{12,4},{13,269},{128,13... | collective-permute-start | bytes 1179656 | tf_op jit(solution)/shard_map/ppermute | solution.py:145
  43.1 3.0 %collective-permute-start.7 = (bf16[2,24,32,128]{3,2,1,0:T(8,128)(2,1)S(1)}, bf16[2,24,32,128]{3,2,1,0:T(8,128)(2,1)S(1)}, u32[]{:S(2)}, u32[]{:S(2)}) collective-permute-start(bf16[2,24,32,128]{3,2,1,0:T(8,128)(2,1)S(1)} %bitcast.29), channel_id=1, source_target_pairs={{0,12},{1,385},{4,0},{5,389},{8,4},{9,393},{12,8},{13,397},{128,14... | collective-permute-start | bytes 1179656 | tf_op jit(solution)/shard_map/ppermute | solution.py:145
  46.1 0.0 collective-permute-done.9.back_ref
  46.1 4.7 %collective-permute-done.8.across_ref = bf16[2,24,32,128]{3,2,1,0:T(8,128)(2,1)S(1)} collective-permute-done((bf16[2,24,32,128]{3,2,1,0:T(8,128)(2,1)S(1)}, bf16[2,24,32,128]{3,2,1,0:T(8,128)(2,1)S(1)}, u32[]{:S(2)}, u32[]{:S(2)}) %collective-permute-start.8) | collective-permute-done | bytes 393248 | tf_op jit(solution)/shard_map/ppermute | solution.py:145
  50.8 1.3 %collective-permute-done.7.ahead_ref = bf16[2,24,32,128]{3,2,1,0:T(8,128)(2,1)S(1)} collective-permute-done((bf16[2,24,32,128]{3,2,1,0:T(8,128)(2,1)S(1)}, bf16[2,24,32,128]{3,2,1,0:T(8,128)(2,1)S(1)}, u32[]{:S(2)}, u32[]{:S(2)}) %collective-permute-start.7) | collective-permute-done | bytes 393248 | tf_op jit(solution)/shard_map/ppermute | solution.py:145
  52.1 0.1 shard_map.66
  52.2 3.1 %collective-permute-start.11 = (bf16[96,32,128]{2,1,0:T(8,128)(2,1)S(1)}, bf16[96,32,128]{2,1,0:T(8,128)(2,1)S(1)}, u32[]{:S(2)}, u32[]{:S(2)}) collective-permute-start(bf16[96,32,128]{2,1,0:T(8,128)(2,1)S(1)} %get-tuple-element.26.refs_5_), channel_id=1, source_target_pairs={{0,128},{1,5},{4,132},{5,9},{8,136},{9,13},{12,140},{13,1},{128,25... | collective-permute-start | bytes 2359304 | tf_op jit(solution)/shard_map/ppermute | solution.py:145
  55.4 3.4 %collective-permute-start.13 = (bf16[96,32,128]{2,1,0:T(8,128)(2,1)S(1)}, bf16[96,32,128]{2,1,0:T(8,128)(2,1)S(1)}, u32[]{:S(2)}, u32[]{:S(2)}) collective-permute-start(bf16[96,32,128]{2,1,0:T(8,128)(2,1)S(1)} %get-tuple-element.27.refs_9_), channel_id=1, source_target_pairs={{0,384},{1,13},{4,388},{5,1},{8,392},{9,5},{12,396},{13,9},{128,0}... | collective-permute-start | bytes 2359304 | tf_op jit(solution)/shard_map/ppermute | solution.py:145
  58.7 0.0 copy-done
  58.8 0.0 copy-done.1
  58.8 0.6 shard_map.65
  59.4 5.4 %collective-permute-start.4 = (bf16[4096,128]{1,0:T(8,128)(2,1)S(1)}, bf16[4096,128]{1,0:T(8,128)(2,1)S(1)}, u32[]{:S(2)}, u32[]{:S(2)}) collective-permute-start(bf16[4096,128]{1,0:T(8,128)(2,1)S(1)} %get-tuple-element.22), channel_id=1, source_target_pairs={{0,1},{1,0},{2,3},{3,2},{4,5},{5,4},{6,7},{7,6},{8,9},{9,8},{10,11... | collective-permute-start | bytes 3145736 | tf_op jit(solution)/shard_map/ppermute | solution.py:149
  64.7 8.4 %collective-permute-start.3 = (f32[56,64]{1,0:T(8,128)S(1)}, f32[56,64]{1,0:T(8,128)S(1)}, u32[]{:S(2)}, u32[]{:S(2)}) collective-permute-start(f32[56,64]{1,0:T(8,128)S(1)} %reshape.59.near_ref), channel_id=1, source_target_pairs={{0,2},{2,0},{1,3},{3,1},{4,6},{6,4},{5,7},{7,5},{8,10},{10,8},{9,1... | collective-permute-start | bytes 43016 | tf_op jit(solution)/shard_map/ppermute | solution.py:306
  73.1 4.3 %collective-permute-start.10 = (bf16[96,32,128]{2,1,0:T(8,128)(2,1)S(1)}, bf16[96,32,128]{2,1,0:T(8,128)(2,1)S(1)}, u32[]{:S(2)}, u32[]{:S(2)}) collective-permute-start(bf16[96,32,128]{2,1,0:T(8,128)(2,1)S(1)} %get-tuple-element.26.refs_5_), channel_id=1, source_target_pairs={{0,384},{1,13},{4,388},{5,1},{8,392},{9,5},{12,396},{13,9},{128,0}... | collective-permute-start | bytes 2359304 | tf_op jit(solution)/shard_map/ppermute | solution.py:145
  77.4 0.8 collective-permute-done.3.far_ref
  78.2 4.0 %collective-permute-start.15 = (bf16[96,32,128]{2,1,0:T(8,128)(2,1)S(1)}, bf16[96,32,128]{2,1,0:T(8,128)(2,1)S(1)}, u32[]{:S(2)}, u32[]{:S(2)}) collective-permute-start(bf16[96,32,128]{2,1,0:T(8,128)(2,1)S(1)} %get-tuple-element.27.refs_9_), channel_id=1, source_target_pairs={{0,128},{1,5},{4,132},{5,9},{8,136},{9,13},{12,140},{13,1},{128,25... | collective-permute-start | bytes 2359304 | tf_op jit(solution)/shard_map/ppermute | solution.py:145
  82.2 0.0 collective-permute-done.11.refs_8_
  82.2 2.2 %collective-permute-start.12 = (bf16[96,32,128]{2,1,0:T(8,128)(2,1)S(1)}, bf16[96,32,128]{2,1,0:T(8,128)(2,1)S(1)}, u32[]{:S(2)}, u32[]{:S(2)}) collective-permute-start(bf16[96,32,128]{2,1,0:T(8,128)(2,1)S(1)} %collective-permute-done.11.refs_8_), channel_id=1, source_target_pairs={{0,128},{1,5},{4,132},{5,9},{8,136},{9,13},{12,140},{13,1},{128,25... | collective-permute-start | bytes 2359304 | tf_op jit(solution)/shard_map/ppermute | solution.py:145
  84.5 0.0 collective-permute-done.13.refs_10_
  84.5 4.3 %collective-permute-start.14 = (bf16[96,32,128]{2,1,0:T(8,128)(2,1)S(1)}, bf16[96,32,128]{2,1,0:T(8,128)(2,1)S(1)}, u32[]{:S(2)}, u32[]{:S(2)}) collective-permute-start(bf16[96,32,128]{2,1,0:T(8,128)(2,1)S(1)} %collective-permute-done.13.refs_10_), channel_id=1, source_target_pairs={{0,384},{1,13},{4,388},{5,1},{8,392},{9,5},{12,396},{13,9},{128,0}... | collective-permute-start | bytes 2359304 | tf_op jit(solution)/shard_map/ppermute | solution.py:145
  88.8 0.3 shard_map.64.refs_2_
  89.0 0.0 collective-permute-done.4
  89.0 0.0 collective-permute-done.10.refs_6_
  89.1 3.4 %collective-permute-done.15.refs_12_ = bf16[96,32,128]{2,1,0:T(8,128)(2,1)S(1)} collective-permute-done((bf16[96,32,128]{2,1,0:T(8,128)(2,1)S(1)}, bf16[96,32,128]{2,1,0:T(8,128)(2,1)S(1)}, u32[]{:S(2)}, u32[]{:S(2)}) %collective-permute-start.15) | collective-permute-done | bytes 786464 | tf_op jit(solution)/shard_map/ppermute | solution.py:145
  92.4 8.4 %collective-permute-done.12.refs_7_ = bf16[96,32,128]{2,1,0:T(8,128)(2,1)S(1)} collective-permute-done((bf16[96,32,128]{2,1,0:T(8,128)(2,1)S(1)}, bf16[96,32,128]{2,1,0:T(8,128)(2,1)S(1)}, u32[]{:S(2)}, u32[]{:S(2)}) %collective-permute-start.12) | collective-permute-done | bytes 786464 | tf_op jit(solution)/shard_map/ppermute | solution.py:145
  100.8 0.0 collective-permute-done.14.refs_11_
  100.8 11.6 %shard_map.67 = (f32[64,64,128]{2,1,0:T(8,128)S(1)}, bf16[64,64,128]{2,1,0:T(8,128)(2,1)S(1)}) custom-call(s32[448]{0:T(512)S(1)} %reshape.58.refs_0_, s32[448]{0:T(512)S(1)} %reshape.56.refs_1_, f32[2,7,64,8]{3,2,1,0:T(8,128)S(1)} %shard_map.64.refs_2_, bf16[64,64,128]{2,1,0:T(8,128)(2,1)S(1)} %bitcast.32, bf16[64,64,128]{2,1,0:T(8,128)(2,1)S(1)} %bitcast.33, ...), custom_call_target="tpu_custom_call" | custom-call | tf_op jit(solution)/shard_map/pallas_call | solution.py:213
  112.4 3.8 %collective-permute-start.16 = (bf16[64,64,128]{2,1,0:T(8,128)(2,1)S(1)}, bf16[64,64,128]{2,1,0:T(8,128)(2,1)S(1)}, u32[]{:S(2)}, u32[]{:S(2)}) collective-permute-start(bf16[64,64,128]{2,1,0:T(8,128)(2,1)S(1)} %get-tuple-element.29), channel_id=1, source_target_pairs={{0,1},{1,0},{2,3},{3,2},{4,5},{5,4},{6,7},{7,6},{8,9},{9,8},{10,11... | collective-permute-start | bytes 3145736 | tf_op jit(solution)/shard_map/ppermute | solution.py:149
  116.3 2.3 %collective-permute-done.16 = bf16[64,64,128]{2,1,0:T(8,128)(2,1)S(1)} collective-permute-done((bf16[64,64,128]{2,1,0:T(8,128)(2,1)S(1)}, bf16[64,64,128]{2,1,0:T(8,128)(2,1)S(1)}, u32[]{:S(2)}, u32[]{:S(2)}) %collective-permute-start.16) | collective-permute-done | bytes 1048608 | tf_op jit(solution)/shard_map/ppermute | solution.py:149
  118.5 2.3 %shard_map.68 = bf16[128,4096]{1,0:T(8,128)(2,1)} custom-call(f32[4096,128]{1,0:T(8,128)S(1)} %bitcast.26, bf16[4096,128]{1,0:T(8,128)(2,1)S(1)} %bitcast.31, bf16[128,4096]{1,0:T(8,128)(2,1)S(1)} %copy-done, f32[1,4096]{1,0:T(1,128)S(1)} %bitcast.35, f32[128,1]{1,0:T(8,128)S(1)} %get-tuple-element.30.inverse_ref), custom_call_target="tpu_custom_call" | custom-call | tf_op jit(solution)/shard_map/pallas_call | solution.py:249
  (5 shorter events, 0.2 us)
Async XLA Ops:
  1.4 22.8 %collective-permute-start.2 = (bf16[4,3,32,128]{3,2,1,0:T(8,128)(2,1)S(1)}, bf16[4,3,32,128]{3,2,1,0:T(8,128)(2,1)S(1)}, u32[]{:S(2)}, u32[]{:S(2)}) collective-permute-start(bf16[4,3,32,128]{3,2,1,0:T(8,128)(2,1)S(1)} %reshape.54), channel_id=1, source_target_pairs={{0,48},{1,83},{16,64},{17,99},{32,80},{33,115},{48,96},{49,1},{64,... | collective-permute-start | bytes 294920 | tf_op jit(solution)/shard_map/ppermute | solution.py:135
  14.3 10.0 %collective-permute-start.1 = (bf16[4,3,32,128]{3,2,1,0:T(8,128)(2,1)S(1)}, bf16[4,3,32,128]{3,2,1,0:T(8,128)(2,1)S(1)}, u32[]{:S(2)}, u32[]{:S(2)}) collective-permute-start(bf16[4,3,32,128]{3,2,1,0:T(8,128)(2,1)S(1)} %reshape.54), channel_id=1, source_target_pairs={{0,32},{1,99},{16,48},{17,115},{32,64},{33,1},{48,80},{49,17},{64,... | collective-permute-start | bytes 294920 | tf_op jit(solution)/shard_map/ppermute | solution.py:135
  18.6 5.7 %collective-permute-start = (bf16[4,3,32,128]{3,2,1,0:T(8,128)(2,1)S(1)}, bf16[4,3,32,128]{3,2,1,0:T(8,128)(2,1)S(1)}, u32[]{:S(2)}, u32[]{:S(2)}) collective-permute-start(bf16[4,3,32,128]{3,2,1,0:T(8,128)(2,1)S(1)} %reshape.54), channel_id=1, source_target_pairs={{0,16},{1,115},{16,32},{17,1},{32,48},{33,17},{48,64},{49,33},{64,... | collective-permute-start | bytes 294920 | tf_op jit(solution)/shard_map/ppermute | solution.py:135
  24.3 34.4 %copy-start = (bf16[128,4096]{1,0:T(8,128)(2,1)S(1)}, bf16[128,4096]{1,0:T(8,128)(2,1)}, u32[]{:S(2)}) copy-start(bf16[128,4096]{1,0:T(8,128)(2,1)} %tokens_ref.3) | copy-start | bytes 3145732
  24.3 34.4 %copy-start.1 = (f32[4096]{0:T(1024)S(1)}, f32[4096]{0:T(1024)}, u32[]{:S(2)}) copy-start(f32[4096]{0:T(1024)} %param.7) | copy-start | bytes 49156
  24.4 10.8 %collective-permute-start.6 = (bf16[3,2,3,32,128]{4,3,2,1,0:T(8,128)(2,1)S(1)}, bf16[3,2,3,32,128]{4,3,2,1,0:T(8,128)(2,1)S(1)}, u32[]{:S(2)}, u32[]{:S(2)}) collective-permute-start(bf16[3,2,3,32,128]{4,3,2,1,0:T(8,128)(2,1)S(1)} %get-tuple-element.32), channel_id=1, source_target_pairs={{0,1},{1,0},{2,3},{3,2},{4,5},{5,4},{6,7},{7,6},{8,9},{9,8},{10,11... | collective-permute-start | bytes 442376 | tf_op jit(solution)/shard_map/ppermute | solution.py:149
  26.5 8.8 %collective-permute-start.5 = (bf16[2,3,32,128]{3,2,1,0:T(8,128)(2,1)S(1)}, bf16[2,3,32,128]{3,2,1,0:T(8,128)(2,1)S(1)}, u32[]{:S(2)}, u32[]{:S(2)}) collective-permute-start(bf16[2,3,32,128]{3,2,1,0:T(8,128)(2,1)S(1)} %get-tuple-element.34), channel_id=1, source_target_pairs={{0,64},{1,67},{16,80},{17,83},{32,96},{33,99},{48,112},{49,115},{6... | collective-permute-start | bytes 147464 | tf_op jit(solution)/shard_map/ppermute | solution.py:135
  35.3 10.7 %collective-permute-start.9 = (bf16[2,24,32,128]{3,2,1,0:T(8,128)(2,1)S(1)}, bf16[2,24,32,128]{3,2,1,0:T(8,128)(2,1)S(1)}, u32[]{:S(2)}, u32[]{:S(2)}) collective-permute-start(bf16[2,24,32,128]{3,2,1,0:T(8,128)(2,1)S(1)} %bitcast.27), channel_id=1, source_target_pairs={{0,4},{1,129},{4,8},{5,133},{8,12},{9,137},{12,0},{13,141},{128,13... | collective-permute-start | bytes 1179656 | tf_op jit(solution)/shard_map/ppermute | solution.py:145
  38.5 12.3 %collective-permute-start.8 = (bf16[2,24,32,128]{3,2,1,0:T(8,128)(2,1)S(1)}, bf16[2,24,32,128]{3,2,1,0:T(8,128)(2,1)S(1)}, u32[]{:S(2)}, u32[]{:S(2)}) collective-permute-start(bf16[2,24,32,128]{3,2,1,0:T(8,128)(2,1)S(1)} %bitcast.28), channel_id=1, source_target_pairs={{0,8},{1,257},{4,12},{5,261},{8,0},{9,265},{12,4},{13,269},{128,13... | collective-permute-start | bytes 1179656 | tf_op jit(solution)/shard_map/ppermute | solution.py:145
  43.1 9.1 %collective-permute-start.7 = (bf16[2,24,32,128]{3,2,1,0:T(8,128)(2,1)S(1)}, bf16[2,24,32,128]{3,2,1,0:T(8,128)(2,1)S(1)}, u32[]{:S(2)}, u32[]{:S(2)}) collective-permute-start(bf16[2,24,32,128]{3,2,1,0:T(8,128)(2,1)S(1)} %bitcast.29), channel_id=1, source_target_pairs={{0,12},{1,385},{4,0},{5,389},{8,4},{9,393},{12,8},{13,397},{128,14... | collective-permute-start | bytes 1179656 | tf_op jit(solution)/shard_map/ppermute | solution.py:145
  52.2 30.0 %collective-permute-start.11 = (bf16[96,32,128]{2,1,0:T(8,128)(2,1)S(1)}, bf16[96,32,128]{2,1,0:T(8,128)(2,1)S(1)}, u32[]{:S(2)}, u32[]{:S(2)}) collective-permute-start(bf16[96,32,128]{2,1,0:T(8,128)(2,1)S(1)} %get-tuple-element.26.refs_5_), channel_id=1, source_target_pairs={{0,128},{1,5},{4,132},{5,9},{8,136},{9,13},{12,140},{13,1},{128,25... | collective-permute-start | bytes 2359304 | tf_op jit(solution)/shard_map/ppermute | solution.py:145
  55.4 29.1 %collective-permute-start.13 = (bf16[96,32,128]{2,1,0:T(8,128)(2,1)S(1)}, bf16[96,32,128]{2,1,0:T(8,128)(2,1)S(1)}, u32[]{:S(2)}, u32[]{:S(2)}) collective-permute-start(bf16[96,32,128]{2,1,0:T(8,128)(2,1)S(1)} %get-tuple-element.27.refs_9_), channel_id=1, source_target_pairs={{0,384},{1,13},{4,388},{5,1},{8,392},{9,5},{12,396},{13,9},{128,0}... | collective-permute-start | bytes 2359304 | tf_op jit(solution)/shard_map/ppermute | solution.py:145
  59.4 29.6 %collective-permute-start.4 = (bf16[4096,128]{1,0:T(8,128)(2,1)S(1)}, bf16[4096,128]{1,0:T(8,128)(2,1)S(1)}, u32[]{:S(2)}, u32[]{:S(2)}) collective-permute-start(bf16[4096,128]{1,0:T(8,128)(2,1)S(1)} %get-tuple-element.22), channel_id=1, source_target_pairs={{0,1},{1,0},{2,3},{3,2},{4,5},{5,4},{6,7},{7,6},{8,9},{9,8},{10,11... | collective-permute-start | bytes 3145736 | tf_op jit(solution)/shard_map/ppermute | solution.py:149
  64.7 13.4 %collective-permute-start.3 = (f32[56,64]{1,0:T(8,128)S(1)}, f32[56,64]{1,0:T(8,128)S(1)}, u32[]{:S(2)}, u32[]{:S(2)}) collective-permute-start(f32[56,64]{1,0:T(8,128)S(1)} %reshape.59.near_ref), channel_id=1, source_target_pairs={{0,2},{2,0},{1,3},{3,1},{4,6},{6,4},{5,7},{7,5},{8,10},{10,8},{9,1... | collective-permute-start | bytes 43016 | tf_op jit(solution)/shard_map/ppermute | solution.py:306
  73.1 15.9 %collective-permute-start.10 = (bf16[96,32,128]{2,1,0:T(8,128)(2,1)S(1)}, bf16[96,32,128]{2,1,0:T(8,128)(2,1)S(1)}, u32[]{:S(2)}, u32[]{:S(2)}) collective-permute-start(bf16[96,32,128]{2,1,0:T(8,128)(2,1)S(1)} %get-tuple-element.26.refs_5_), channel_id=1, source_target_pairs={{0,384},{1,13},{4,388},{5,1},{8,392},{9,5},{12,396},{13,9},{128,0}... | collective-permute-start | bytes 2359304 | tf_op jit(solution)/shard_map/ppermute | solution.py:145
  78.2 14.2 %collective-permute-start.15 = (bf16[96,32,128]{2,1,0:T(8,128)(2,1)S(1)}, bf16[96,32,128]{2,1,0:T(8,128)(2,1)S(1)}, u32[]{:S(2)}, u32[]{:S(2)}) collective-permute-start(bf16[96,32,128]{2,1,0:T(8,128)(2,1)S(1)} %get-tuple-element.27.refs_9_), channel_id=1, source_target_pairs={{0,128},{1,5},{4,132},{5,9},{8,136},{9,13},{12,140},{13,1},{128,25... | collective-permute-start | bytes 2359304 | tf_op jit(solution)/shard_map/ppermute | solution.py:145
  82.2 18.6 %collective-permute-start.12 = (bf16[96,32,128]{2,1,0:T(8,128)(2,1)S(1)}, bf16[96,32,128]{2,1,0:T(8,128)(2,1)S(1)}, u32[]{:S(2)}, u32[]{:S(2)}) collective-permute-start(bf16[96,32,128]{2,1,0:T(8,128)(2,1)S(1)} %collective-permute-done.11.refs_8_), channel_id=1, source_target_pairs={{0,128},{1,5},{4,132},{5,9},{8,136},{9,13},{12,140},{13,1},{128,25... | collective-permute-start | bytes 2359304 | tf_op jit(solution)/shard_map/ppermute | solution.py:145
  84.5 16.4 %collective-permute-start.14 = (bf16[96,32,128]{2,1,0:T(8,128)(2,1)S(1)}, bf16[96,32,128]{2,1,0:T(8,128)(2,1)S(1)}, u32[]{:S(2)}, u32[]{:S(2)}) collective-permute-start(bf16[96,32,128]{2,1,0:T(8,128)(2,1)S(1)} %collective-permute-done.13.refs_10_), channel_id=1, source_target_pairs={{0,384},{1,13},{4,388},{5,1},{8,392},{9,5},{12,396},{13,9},{128,0}... | collective-permute-start | bytes 2359304 | tf_op jit(solution)/shard_map/ppermute | solution.py:145
  112.4 6.1 %collective-permute-start.16 = (bf16[64,64,128]{2,1,0:T(8,128)(2,1)S(1)}, bf16[64,64,128]{2,1,0:T(8,128)(2,1)S(1)}, u32[]{:S(2)}, u32[]{:S(2)}) collective-permute-start(bf16[64,64,128]{2,1,0:T(8,128)(2,1)S(1)} %get-tuple-element.29), channel_id=1, source_target_pairs={{0,1},{1,0},{2,3},{3,2},{4,5},{5,4},{6,7},{7,6},{8,9},{9,8},{10,11... | collective-permute-start | bytes 3145736 | tf_op jit(solution)/shard_map/ppermute | solution.py:149

commit v3 on v2

--- a/solution.py
+++ b/solution.py
@@ -10,7 +10,8 @@
 HALF = BLOCK // 2
 EPS = 1e-05
 LANES = 128
-GROUP = 8
+GROUP = 28
+ROWS = 32
 NX, NY, NZ = 4, 4, 8
 SIDE = 4
 AXES = ("y", "zl", "x", "zh", "core")
@@ -31,81 +32,122 @@
         feat_ref[at : at + LANES, :] = scaled[:, at : at + LANES].T
 
 
-def sparse_kernel(columns, per_column, tile_ref, row_ref, unit_ref, mine_ref, other_ref, *refs):
-    parts, (keep_ref, send_ref, away_ref, w_ref, sems) = refs[:8], refs[8:]
-    count = mine_ref.shape[2]
+def invert_kernel(columns, per_column, tile_ref, row_ref, back_tile_ref, back_column_ref, count_ref):
+    runs = 2
+    blank = runs * SIDE * SIDE * NZ * 3
+    spots = back_tile_ref.shape[0]
+
+    def clear(i, carry):
+        for j in range(4):
+            back_tile_ref[4 * i + j] = blank
+            back_column_ref[4 * i + j] = 0
+        count_ref[i] = 0
+        return carry
+
+    lax.fori_loop(0, spots // 4, clear, 0)
+
+    def note(column, carry):
+        for k in range(per_column):
+            at = column * per_column + k
+            line = row_ref[at] + jnp.where(column < columns, 0, spots // 4 // runs)
+            seen = count_ref[line]
+            back_tile_ref[line * 4 + seen] = tile_ref[at]
+            back_column_ref[line * 4 + seen] = column
+            count_ref[line] = seen + 1
+        return carry
+
+    lax.fori_loop(0, runs * columns, note, 0)
+
+
+def invert_call(columns, per_column, row_blocks, places, rows):
+    spots = 2 * row_blocks * 4
+
+    def body(*refs):
+        invert_kernel(columns, per_column, *refs)
+
+    return pl.pallas_call(
+        body,
+        out_shape=[jax.ShapeDtypeStruct((spots,), jnp.int32)] * 2,
+        in_specs=[SMEM, SMEM],
+        out_specs=[SMEM, SMEM],
+        scratch_shapes=[pltpu.SMEM((spots // 4,), jnp.int32)],
+        compiler_params=pltpu.CompilerParams(vmem_limit_bytes=1 << 20),
+    )(places, rows)
+
+
+def sparse_kernel(
+    columns, per_column, tile_ref, row_ref, back_tile_ref, back_column_ref, unit_ref, mine_ref,
+    other_ref, *refs
+):
+    parts, (keep_ref, send_ref, grad_ref, w_ref, sems) = refs[:8], refs[8:]
+    row_blocks, _, count = mine_ref.shape
     size = parts[0].shape[0]
     copies = []
     for i, source in enumerate(parts):
         run, at = i // SIDE, i % SIDE
-        target = w_ref.at[run, pl.ds(at * size, size)]
+        target = w_ref.at[pl.ds(i * size, size)]
         copies.append(pltpu.make_async_copy(source, target, sems.at[run, at]))
     for copy in copies:
         copy.start()
-    keep_ref[...] = jnp.zeros_like(keep_ref)
-    away_ref[...] = jnp.zeros_like(away_ref)
-    blank = jnp.zeros((BLOCK, 2 * count), jnp.bfloat16)
-
-    def work(run):
-        def group(g, carry):
-            first = (run * columns + g * GROUP) * per_column
-            units = unit_ref[run, g]
-
-            def forward(j):
-                at = first + j * per_column
-                rows = [row_ref[at + k] for k in range(per_column)]
-                stack = jnp.concatenate(
-                    [w_ref[run, tile_ref[at + k]] for k in range(per_column)], axis=0
-                )
-                turned = stack.T
-                lhs = jnp.concatenate([turned[:BLOCK], turned[BLOCK:]], axis=1)
-                mine = [mine_ref[r] for r in rows]
-                other = [other_ref[r] for r in rows]
-                rhs = jnp.concatenate(
-                    [
-                        jnp.concatenate([p[:HALF] for p in side] + [p[HALF:] for p in side], axis=0)
-                        for side in (mine, other)
-                    ],
-                    axis=1,
-                )
-                preact = jnp.dot(lhs, rhs, preferred_element_type=jnp.float32)
-                gating = jax.nn.sigmoid(preact)
-                grad_act = units[:, j : j + 1] * (preact * gating)
-                grad_pre = grad_act * (gating * (1.0 + preact * (1.0 - gating)))
-                return rows, stack, grad_pre.astype(jnp.bfloat16)
-
-            def backward(rows, stack, grad_pre):
-                upper = jnp.dot(
-                    stack,
-                    jnp.concatenate([grad_pre, blank], axis=0),
-                    preferred_element_type=jnp.float32,
-                )
-                lower = jnp.dot(
-                    stack,
-                    jnp.concatenate([blank, grad_pre], axis=0),
-                    preferred_element_type=jnp.float32,
-                )
-                for ref, lanes in ((keep_ref, slice(0, count)), (away_ref, slice(count, None))):
-                    sums = []
-                    for k in range(per_column):
-                        span = slice(k * HALF, (k + 1) * HALF)
-                        term = jnp.concatenate([upper[span, lanes], lower[span, lanes]], axis=0)
-                        sums.append(ref[rows[k]] + term)
-                    for k in range(per_column):
-                        ref[rows[k]] = sums[k]
-
-            held = [forward(j) for j in range(GROUP)]
-            for piece in held:
-                backward(*piece)
-            return carry
-
-        lax.fori_loop(0, columns // GROUP, group, 0)
-
+    w_ref[len(parts) * size] = jnp.zeros(w_ref.shape[1:], w_ref.dtype)
+
+    def forward(g, j):
+        at = (g * GROUP + j) * per_column
+        rows = [row_ref[at + k] for k in range(per_column)]
+        tiles = [w_ref[tile_ref[at + k]] for k in range(per_column)]
+        turned = jnp.concatenate(tiles, axis=0).T
+        lhs = jnp.concatenate([turned[:BLOCK], turned[BLOCK:]], axis=1)
+        mine = [mine_ref[r] for r in rows]
+        other = [other_ref[r] for r in rows]
+        rhs = jnp.concatenate(
+            [
+                jnp.concatenate([p[:HALF] for p in side] + [p[HALF:] for p in side], axis=0)
+                for side in (mine, other)
+            ],
+            axis=1,
+        )
+        preact = jnp.dot(lhs, rhs, preferred_element_type=jnp.float32)
+        gating = jax.nn.sigmoid(preact)
+        grad_act = unit_ref[g][:, j : j + 1] * (preact * gating)
+        grad_pre = grad_act * (gating * (1.0 + preact * (1.0 - gating)))
+        grad_ref[g * GROUP + j] = grad_pre.astype(jnp.bfloat16)
+
+    def ahead(g, carry):
+        for j in range(GROUP):
+            forward(g, j)
+        return carry
+
+    left = lax.broadcasted_iota(jnp.int32, (HALF, 2 * BLOCK), 1) < BLOCK
+
+    def backward(row):
+        total = None
+        for run in range(2):
+            at = (run * row_blocks + row) * 4
+            upper, lower = [], []
+            for k in range(0, 4, 2):
+                first, second = w_ref[back_tile_ref[at + k]], w_ref[back_tile_ref[at + k + 1]]
+                upper.append(jnp.where(left, first, pltpu.roll(second, BLOCK, 1)))
+                lower.append(jnp.where(left, pltpu.roll(first, BLOCK, 1), second))
+            lhs = jnp.concatenate(
+                [jnp.concatenate(upper, axis=1), jnp.concatenate(lower, axis=1)], axis=0
+            )
+            rhs = jnp.concatenate([grad_ref[back_column_ref[at + k]] for k in range(4)], axis=0)
+            part = jnp.dot(lhs, rhs, preferred_element_type=jnp.float32)
+            total = part if total is None else total + part
+        keep_ref[row] = total[:, :count]
+        send_ref[row] = total[:, count:].astype(jnp.bfloat16)
+
+    def back(g, carry):
+        for j in range(ROWS):
+            backward(g * ROWS + j)
+        return carry
+
+    groups = columns // GROUP
     for run in range(2):
-        for copy in copies[4 * run : 4 * run + 4]:
+        for copy in copies[run * SIDE : (run + 1) * SIDE]:
             copy.wait()
-        work(run)
-    send_ref[...] = away_ref[...].astype(jnp.bfloat16)
+        lax.fori_loop(run * groups, (run + 1) * groups, ahead, 0)
+    lax.fori_loop(0, row_blocks // ROWS, back, 0)
 
 
 def close_kernel(keep_ref, came_ref, tokens_ref, gain_ref, inverse_ref, out_ref, grad_ref):
@@ -204,7 +246,7 @@
     return ((second * SIDE + first) * NZ + step_z) * slots + place
 
 
-def sparse_call(columns, per_column, places, rows, units, mine, other, tiles):
+def sparse_call(columns, per_column, places, rows, back_places, back_columns, units, mine, other, tiles):
     row_blocks, _, count = mine.shape
 
     def body(*refs):
@@ -216,16 +258,16 @@
             pltpu.VMEM((row_blocks, BLOCK, count), jnp.float32),
             pltpu.VMEM((row_blocks, BLOCK, count), jnp.bfloat16),
         ),
-        in_specs=[SMEM, SMEM] + [VMEM] * 11,
+        in_specs=[SMEM] * 4 + [VMEM] * 11,
         out_specs=(VMEM, VMEM),
         scratch_shapes=[
-            pltpu.VMEM((row_blocks, BLOCK, count), jnp.float32),
-            pltpu.VMEM((2, SIDE * tiles[0].shape[0], HALF, 2 * BLOCK), jnp.bfloat16),
+            pltpu.VMEM((2 * columns, BLOCK, 2 * count), jnp.bfloat16),
+            pltpu.VMEM((len(tiles) * tiles[0].shape[0] + 1, HALF, 2 * BLOCK), jnp.bfloat16),
             pltpu.SemaphoreType.DMA((2, 4)),
         ],
         compiler_params=pltpu.CompilerParams(vmem_limit_bytes=14 << 20),
     )(
-        places, rows, on_chip(units), on_chip(mine), on_chip(other),
+        places, rows, back_places, back_columns, on_chip(units), on_chip(mine), on_chip(other),
         *map(on_chip, tiles),
     )
 
@@ -265,14 +307,14 @@
     for run in range(2):
         turned = jnp.where(high == run, near, far).T
         for g in range(groups):
-            units_ref[run, g] = turned[:, g * GROUP : (g + 1) * GROUP]
+            units_ref[run * groups + g] = turned[:, g * GROUP : (g + 1) * GROUP]
 
 
 def unit_call(high, near, far):
     columns, block = near.shape
     return pl.pallas_call(
         unit_kernel,
-        out_shape=pltpu.VMEM((2, columns // GROUP, block, GROUP), jnp.float32),
+        out_shape=pltpu.VMEM((2 * columns // GROUP, block, GROUP), jnp.float32),
         in_specs=[SMEM, VMEM, VMEM],
         out_specs=VMEM,
         compiler_params=pltpu.CompilerParams(vmem_limit_bytes=1 << 20),
@@ -296,7 +338,9 @@
         return lax.dynamic_index_in_dim(paired, core, 1, keepdims=False).reshape(-1)
 
     rows = of_runs(block_rows)
-    places = of_runs(tile_places(block_slot, slots, y, zl, x, core))
+    places = tile_places(block_slot, slots, y, zl, x, core).reshape(runs, columns * per_column)
+    second = jnp.arange(runs)[:, None] // 2 * (NX * NY * NZ * slots)
+    places = of_runs(places + second)
     near = penalty.reshape(columns, BLOCK)
     own = pack_tiles(weight_tiles)
     tiles, (rows, places, near, high) = gather_tiles(own, core, (rows, places, near, zh.reshape(1)))
@@ -306,8 +350,9 @@
     distant = lax.ppermute(near, "zh", [(0, 1), (1, 0)])
     units = unit_call(high, near, distant)
     blocks = (width // BLOCK, BLOCK, count)
+    back = invert_call(columns, per_column, width // BLOCK, places, rows)
     keep, send = sparse_call(
-        columns, per_column, places, rows, units, features.reshape(blocks), other.reshape(blocks), tiles
+        columns, per_column, places, rows, *back, units, features.reshape(blocks), other.reshape(blocks), tiles
     )
     came = swap_cores(send)
     return close_call(keep, came, tokens, gain, inverse)
@@ -317,6 +362,4 @@
     fine = Mesh(mesh.devices.reshape(NY, NZ, NX, 2, 2), AXES)
     placed = (P(AXES, None), P(), P(("zh", "core")), P(None, ("y", "zl", "x"), None), P(), P())
 
-    return jax.shard_map(
-        on_device, mesh=fine, in_specs=placed, out_specs=P(AXES, None), check_vma=False
-    )
+    return jax.shard_map(on_device, mesh=fine, in_specs=placed, out_specs=P(AXES, None), check_vma=False)

time: 122 us -> 119 us (0.975)
  waiting for transfers between devices: 24.6 us -> 18.8 us
  Pallas kernels: 14.8 us -> 17.1 us
    ppermute x9, waiting for transfers between devices: 17.9 us -> 11.8 us  [along_side(): return lax.ppermute(v, ('y', 'x', 'core'), pairs)]
    pallas_call x1 -> x2, Pallas kernels: 0.27 us -> 6.34 us  [the longest x1 6.18 us: invert_call(): pl.pallas_call(body, out_shape=[jax.ShapeDtypeStruct((spots,), jnp.int32)...]
    pallas_call x1, Pallas kernels: 11.6 us -> 7.93 us  [sparse_call(): pl.pallas_call(body, out_shape=(pltpu.VMEM((row_blocks, BLOCK, count), jn...]
  transfers between devices with their start and end apart: 17 -> 17, of which waited for: 7 -> 6; matrix products, arithmetic and copies ran while one was open for 3% -> 3% of each run, Pallas kernels for 1% -> 6%
where the time goes in v3:
time: 119 us; the launch traced here: 117 us
  starting transfers between devices  76.2 us (64%)
  waiting for transfers between devices  18.8 us (16%)
  Pallas kernels  17.1 us (14%)
  local copies, waits for them, and re-layouts  3.82 us (3%)
    ppermute x9, starting transfers between devices, along_side(): return lax.ppermute(v, ('y', 'x', 'core'), pairs)  32 us
    ppermute x4, starting transfers between devices, along_z(): return lax.ppermute(v, ('zl', 'zh', 'core'), pairs)  24.7 us
    ppermute x9, waiting for transfers between devices, along_side(): return lax.ppermute(v, ('y', 'x', 'core'), pairs)  11.8 us
    ppermute x3, starting transfers between devices, swap_cores(): return lax.ppermute(v, 'core', [(0, 1), (1, 0)])  11.3 us
    ppermute x1, starting transfers between devices, on_device(): distant = lax.ppermute(near, 'zh', [(0, 1), (1, 0)])  8.18 us
    pallas_call x1, Pallas kernels, sparse_call(): pl.pallas_call(body, out_shape=(pltpu.VMEM((row_blocks, BLOCK, count), jn...  7.93 us
    pallas_call x1, Pallas kernels, invert_call(): pl.pallas_call(body, out_shape=[jax.ShapeDtypeStruct((spots,), jnp.int32)...  6.18 us
    ppermute x4, waiting for transfers between devices, along_z(): return lax.ppermute(v, ('zl', 'zh', 'core'), pairs)  3.83 us
  transfers between devices with their start and end apart: 17, of which 6 were waited for; matrix products, arithmetic and copies ran while one was open for 3% of the time, Pallas kernels for 6%

profile of v3, /device:TPU:1, one launch (start us, length us, event | category | flops | bytes accessed | tf_op | source)
XLA Modules:
  0.0 117.2 jit_solution(1376445186115793107)
XLA Ops:
  0.0 1.1 reshape.101
  1.1 0.2 copy.15
  1.3 0.1 reshape.102
  1.4 12.8 %collective-permute-start.2 = (bf16[4,3,32,128]{3,2,1,0:T(8,128)(2,1)S(1)}, bf16[4,3,32,128]{3,2,1,0:T(8,128)(2,1)S(1)}, u32[]{:S(2)}, u32[]{:S(2)}) collective-permute-start(bf16[4,3,32,128]{3,2,1,0:T(8,128)(2,1)S(1)} %reshape.102), channel_id=1, source_target_pairs={{0,48},{1,83},{16,64},{17,99},{32,80},{33,115},{48,96},{49,1},{64,... | collective-permute-start | bytes 294920 | tf_op jit(solution)/shard_map/ppermute | solution.py:177
  14.3 4.3 %collective-permute-start.1 = (bf16[4,3,32,128]{3,2,1,0:T(8,128)(2,1)S(1)}, bf16[4,3,32,128]{3,2,1,0:T(8,128)(2,1)S(1)}, u32[]{:S(2)}, u32[]{:S(2)}) collective-permute-start(bf16[4,3,32,128]{3,2,1,0:T(8,128)(2,1)S(1)} %reshape.102), channel_id=1, source_target_pairs={{0,32},{1,99},{16,48},{17,115},{32,64},{33,1},{48,80},{49,17},{64,... | collective-permute-start | bytes 294920 | tf_op jit(solution)/shard_map/ppermute | solution.py:177
  18.6 2.6 %collective-permute-start = (bf16[4,3,32,128]{3,2,1,0:T(8,128)(2,1)S(1)}, bf16[4,3,32,128]{3,2,1,0:T(8,128)(2,1)S(1)}, u32[]{:S(2)}, u32[]{:S(2)}) collective-permute-start(bf16[4,3,32,128]{3,2,1,0:T(8,128)(2,1)S(1)} %reshape.102), channel_id=1, source_target_pairs={{0,16},{1,115},{16,32},{17,1},{32,48},{33,17},{48,64},{49,33},{64,... | collective-permute-start | bytes 294920 | tf_op jit(solution)/shard_map/ppermute | solution.py:177
  21.2 0.1 reshape_reshape.3
  21.4 0.8 reshape.107.near_ref
  22.2 0.7 fusion.9
  22.9 0.1 copy.12
  23.0 0.1 reshape.105
  23.1 0.8 copy.11
  24.0 0.1 reshape.103
  24.1 0.1 constant_dynamic-slice_fusion
  24.2 0.1 fusion.14
  24.2 0.1 reshape.106.refs_0_
  24.3 0.1 reshape.104.refs_1_
  24.4 0.0 collective-permute-done.2
  24.4 0.0 collective-permute-done.1
  24.4 0.0 collective-permute-done
  24.5 0.0 copy-start
  24.5 0.0 copy-start.1
  24.5 2.1 %collective-permute-start.6 = (bf16[3,2,3,32,128]{4,3,2,1,0:T(8,128)(2,1)S(1)}, bf16[3,2,3,32,128]{4,3,2,1,0:T(8,128)(2,1)S(1)}, u32[]{:S(2)}, u32[]{:S(2)}) collective-permute-start(bf16[3,2,3,32,128]{4,3,2,1,0:T(8,128)(2,1)S(1)} %get-tuple-element.36), channel_id=1, source_target_pairs={{0,1},{1,0},{2,3},{3,2},{4,5},{5,4},{6,7},{7,6},{8,9},{9,8},{10,11... | collective-permute-start | bytes 442376 | tf_op jit(solution)/shard_map/ppermute | solution.py:191
  26.6 4.9 %collective-permute-start.5 = (bf16[2,3,32,128]{3,2,1,0:T(8,128)(2,1)S(1)}, bf16[2,3,32,128]{3,2,1,0:T(8,128)(2,1)S(1)}, u32[]{:S(2)}, u32[]{:S(2)}) collective-permute-start(bf16[2,3,32,128]{3,2,1,0:T(8,128)(2,1)S(1)} %get-tuple-element.38), channel_id=1, source_target_pairs={{0,64},{1,67},{16,80},{17,83},{32,96},{33,99},{48,112},{49,115},{6... | collective-permute-start | bytes 147464 | tf_op jit(solution)/shard_map/ppermute | solution.py:177
  31.6 3.8 %collective-permute-done.5 = bf16[2,3,32,128]{3,2,1,0:T(8,128)(2,1)S(1)} collective-permute-done((bf16[2,3,32,128]{3,2,1,0:T(8,128)(2,1)S(1)}, bf16[2,3,32,128]{3,2,1,0:T(8,128)(2,1)S(1)}, u32[]{:S(2)}, u32[]{:S(2)}) %collective-permute-start.5) | collective-permute-done | bytes 49184 | tf_op jit(solution)/shard_map/ppermute | solution.py:177
  35.4 0.0 collective-permute-done.6
  35.4 0.1 maximum_bitcast_fusion
  35.5 3.2 %collective-permute-start.9 = (bf16[2,24,32,128]{3,2,1,0:T(8,128)(2,1)S(1)}, bf16[2,24,32,128]{3,2,1,0:T(8,128)(2,1)S(1)}, u32[]{:S(2)}, u32[]{:S(2)}) collective-permute-start(bf16[2,24,32,128]{3,2,1,0:T(8,128)(2,1)S(1)} %bitcast.27), channel_id=1, source_target_pairs={{0,4},{1,129},{4,8},{5,133},{8,12},{9,137},{12,0},{13,141},{128,13... | collective-permute-start | bytes 1179656 | tf_op jit(solution)/shard_map/ppermute | solution.py:187
  38.7 4.5 %collective-permute-start.8 = (bf16[2,24,32,128]{3,2,1,0:T(8,128)(2,1)S(1)}, bf16[2,24,32,128]{3,2,1,0:T(8,128)(2,1)S(1)}, u32[]{:S(2)}, u32[]{:S(2)}) collective-permute-start(bf16[2,24,32,128]{3,2,1,0:T(8,128)(2,1)S(1)} %bitcast.28), channel_id=1, source_target_pairs={{0,8},{1,257},{4,12},{5,261},{8,0},{9,265},{12,4},{13,269},{128,13... | collective-permute-start | bytes 1179656 | tf_op jit(solution)/shard_map/ppermute | solution.py:187
  43.2 3.0 %collective-permute-start.7 = (bf16[2,24,32,128]{3,2,1,0:T(8,128)(2,1)S(1)}, bf16[2,24,32,128]{3,2,1,0:T(8,128)(2,1)S(1)}, u32[]{:S(2)}, u32[]{:S(2)}) collective-permute-start(bf16[2,24,32,128]{3,2,1,0:T(8,128)(2,1)S(1)} %bitcast.29), channel_id=1, source_target_pairs={{0,12},{1,385},{4,0},{5,389},{8,4},{9,393},{12,8},{13,397},{128,14... | collective-permute-start | bytes 1179656 | tf_op jit(solution)/shard_map/ppermute | solution.py:187
  46.2 0.0 collective-permute-done.9.back_ref
  46.2 4.7 %collective-permute-done.8.across_ref = bf16[2,24,32,128]{3,2,1,0:T(8,128)(2,1)S(1)} collective-permute-done((bf16[2,24,32,128]{3,2,1,0:T(8,128)(2,1)S(1)}, bf16[2,24,32,128]{3,2,1,0:T(8,128)(2,1)S(1)}, u32[]{:S(2)}, u32[]{:S(2)}) %collective-permute-start.8) | collective-permute-done | bytes 393248 | tf_op jit(solution)/shard_map/ppermute | solution.py:187
  51.0 1.3 %collective-permute-done.7.ahead_ref = bf16[2,24,32,128]{3,2,1,0:T(8,128)(2,1)S(1)} collective-permute-done((bf16[2,24,32,128]{3,2,1,0:T(8,128)(2,1)S(1)}, bf16[2,24,32,128]{3,2,1,0:T(8,128)(2,1)S(1)}, u32[]{:S(2)}, u32[]{:S(2)}) %collective-permute-start.7) | collective-permute-done | bytes 393248 | tf_op jit(solution)/shard_map/ppermute | solution.py:187
  52.3 0.1 shard_map.67
  52.4 3.1 %collective-permute-start.11 = (bf16[96,32,128]{2,1,0:T(8,128)(2,1)S(1)}, bf16[96,32,128]{2,1,0:T(8,128)(2,1)S(1)}, u32[]{:S(2)}, u32[]{:S(2)}) collective-permute-start(bf16[96,32,128]{2,1,0:T(8,128)(2,1)S(1)} %get-tuple-element.30.refs_7_), channel_id=1, source_target_pairs={{0,128},{1,5},{4,132},{5,9},{8,136},{9,13},{12,140},{13,1},{128,25... | collective-permute-start | bytes 2359304 | tf_op jit(solution)/shard_map/ppermute | solution.py:187
  55.5 3.4 %collective-permute-start.13 = (bf16[96,32,128]{2,1,0:T(8,128)(2,1)S(1)}, bf16[96,32,128]{2,1,0:T(8,128)(2,1)S(1)}, u32[]{:S(2)}, u32[]{:S(2)}) collective-permute-start(bf16[96,32,128]{2,1,0:T(8,128)(2,1)S(1)} %get-tuple-element.31.refs_11_), channel_id=1, source_target_pairs={{0,384},{1,13},{4,388},{5,1},{8,392},{9,5},{12,396},{13,9},{128,0}... | collective-permute-start | bytes 2359304 | tf_op jit(solution)/shard_map/ppermute | solution.py:187
  58.9 0.0 copy-done
  58.9 0.0 copy-done.1
  58.9 0.6 shard_map.66
  59.5 5.4 %collective-permute-start.4 = (bf16[4096,128]{1,0:T(8,128)(2,1)S(1)}, bf16[4096,128]{1,0:T(8,128)(2,1)S(1)}, u32[]{:S(2)}, u32[]{:S(2)}) collective-permute-start(bf16[4096,128]{1,0:T(8,128)(2,1)S(1)} %get-tuple-element.26), channel_id=1, source_target_pairs={{0,1},{1,0},{2,3},{3,2},{4,5},{5,4},{6,7},{7,6},{8,9},{9,8},{10,11... | collective-permute-start | bytes 3145736 | tf_op jit(solution)/shard_map/ppermute | solution.py:191
  64.9 8.2 %collective-permute-start.3 = (f32[56,64]{1,0:T(8,128)S(1)}, f32[56,64]{1,0:T(8,128)S(1)}, u32[]{:S(2)}, u32[]{:S(2)}) collective-permute-start(f32[56,64]{1,0:T(8,128)S(1)} %reshape.107.near_ref), channel_id=1, source_target_pairs={{0,2},{2,0},{1,3},{3,1},{4,6},{6,4},{5,7},{7,5},{8,10},{10,8},{9,1... | collective-permute-start | bytes 43016 | tf_op jit(solution)/shard_map/ppermute | solution.py:350
  73.1 4.3 %collective-permute-start.10 = (bf16[96,32,128]{2,1,0:T(8,128)(2,1)S(1)}, bf16[96,32,128]{2,1,0:T(8,128)(2,1)S(1)}, u32[]{:S(2)}, u32[]{:S(2)}) collective-permute-start(bf16[96,32,128]{2,1,0:T(8,128)(2,1)S(1)} %get-tuple-element.30.refs_7_), channel_id=1, source_target_pairs={{0,384},{1,13},{4,388},{5,1},{8,392},{9,5},{12,396},{13,9},{128,0}... | collective-permute-start | bytes 2359304 | tf_op jit(solution)/shard_map/ppermute | solution.py:187
  77.4 0.9 collective-permute-done.3.far_ref
  78.4 4.0 %collective-permute-start.15 = (bf16[96,32,128]{2,1,0:T(8,128)(2,1)S(1)}, bf16[96,32,128]{2,1,0:T(8,128)(2,1)S(1)}, u32[]{:S(2)}, u32[]{:S(2)}) collective-permute-start(bf16[96,32,128]{2,1,0:T(8,128)(2,1)S(1)} %get-tuple-element.31.refs_11_), channel_id=1, source_target_pairs={{0,128},{1,5},{4,132},{5,9},{8,136},{9,13},{12,140},{13,1},{128,25... | collective-permute-start | bytes 2359304 | tf_op jit(solution)/shard_map/ppermute | solution.py:187
  82.4 0.0 collective-permute-done.11.refs_10_
  82.4 2.2 %collective-permute-start.12 = (bf16[96,32,128]{2,1,0:T(8,128)(2,1)S(1)}, bf16[96,32,128]{2,1,0:T(8,128)(2,1)S(1)}, u32[]{:S(2)}, u32[]{:S(2)}) collective-permute-start(bf16[96,32,128]{2,1,0:T(8,128)(2,1)S(1)} %collective-permute-done.11.refs_10_), channel_id=1, source_target_pairs={{0,128},{1,5},{4,132},{5,9},{8,136},{9,13},{12,140},{13,1},{128,25... | collective-permute-start | bytes 2359304 | tf_op jit(solution)/shard_map/ppermute | solution.py:187
  84.7 0.0 collective-permute-done.13.refs_12_
  84.7 4.3 %collective-permute-start.14 = (bf16[96,32,128]{2,1,0:T(8,128)(2,1)S(1)}, bf16[96,32,128]{2,1,0:T(8,128)(2,1)S(1)}, u32[]{:S(2)}, u32[]{:S(2)}) collective-permute-start(bf16[96,32,128]{2,1,0:T(8,128)(2,1)S(1)} %collective-permute-done.13.refs_12_), channel_id=1, source_target_pairs={{0,384},{1,13},{4,388},{5,1},{8,392},{9,5},{12,396},{13,9},{128,0}... | collective-permute-start | bytes 2359304 | tf_op jit(solution)/shard_map/ppermute | solution.py:187
  88.9 6.2 %shard_map.64 = (s32[512]{0:T(512)S(1)}, s32[512]{0:T(512)S(1)}) custom-call(s32[448]{0:T(512)S(1)} %reshape.106.refs_0_, s32[448]{0:T(512)S(1)} %reshape.104.refs_1_), custom_call_target="tpu_custom_call" | custom-call | tf_op jit(solution)/shard_map/pallas_call | solution.py:68
  95.1 0.2 shard_map.65.refs_4_
  95.3 0.0 collective-permute-done.4
  95.3 0.0 collective-permute-done.10.refs_8_
  95.3 0.0 collective-permute-done.15.refs_14_
  95.3 5.7 %collective-permute-done.12.refs_9_ = bf16[96,32,128]{2,1,0:T(8,128)(2,1)S(1)} collective-permute-done((bf16[96,32,128]{2,1,0:T(8,128)(2,1)S(1)}, bf16[96,32,128]{2,1,0:T(8,128)(2,1)S(1)}, u32[]{:S(2)}, u32[]{:S(2)}) %collective-permute-start.12) | collective-permute-done | bytes 786464 | tf_op jit(solution)/shard_map/ppermute | solution.py:187
  101.0 0.0 collective-permute-done.14.refs_13_
  101.0 7.9 %shard_map.68 = (f32[64,64,128]{2,1,0:T(8,128)S(1)}, bf16[64,64,128]{2,1,0:T(8,128)(2,1)S(1)}) custom-call(s32[448]{0:T(512)S(1)} %reshape.106.refs_0_, s32[448]{0:T(512)S(1)} %reshape.104.refs_1_, s32[512]{0:T(512)S(1)} %get-tuple-element.22.refs_2_, s32[512]{0:T(512)S(1)} %get-tuple-element.23.refs_3_, f32[4,64,28]{2,1,0:T(8,128)S(1)} %shard_map.65.refs_4_, ...), custom_call_target="tpu_custom_call" | custom-call | tf_op jit(solution)/shard_map/pallas_call | solution.py:255
  109.0 3.8 %collective-permute-start.16 = (bf16[64,64,128]{2,1,0:T(8,128)(2,1)S(1)}, bf16[64,64,128]{2,1,0:T(8,128)(2,1)S(1)}, u32[]{:S(2)}, u32[]{:S(2)}) collective-permute-start(bf16[64,64,128]{2,1,0:T(8,128)(2,1)S(1)} %get-tuple-element.33), channel_id=1, source_target_pairs={{0,1},{1,0},{2,3},{3,2},{4,5},{5,4},{6,7},{7,6},{8,9},{9,8},{10,11... | collective-permute-start | bytes 3145736 | tf_op jit(solution)/shard_map/ppermute | solution.py:191
  112.8 2.3 %collective-permute-done.16 = bf16[64,64,128]{2,1,0:T(8,128)(2,1)S(1)} collective-permute-done((bf16[64,64,128]{2,1,0:T(8,128)(2,1)S(1)}, bf16[64,64,128]{2,1,0:T(8,128)(2,1)S(1)}, u32[]{:S(2)}, u32[]{:S(2)}) %collective-permute-start.16) | collective-permute-done | bytes 1048608 | tf_op jit(solution)/shard_map/ppermute | solution.py:191
  115.1 2.1 %shard_map.69 = bf16[128,4096]{1,0:T(8,128)(2,1)} custom-call(f32[4096,128]{1,0:T(8,128)S(1)} %bitcast.26, bf16[4096,128]{1,0:T(8,128)(2,1)S(1)} %bitcast.33, bf16[128,4096]{1,0:T(8,128)(2,1)S(1)} %copy-done, f32[1,4096]{1,0:T(1,128)S(1)} %bitcast.35, f32[128,1]{1,0:T(8,128)S(1)} %get-tuple-element.34.inverse_ref), custom_call_target="tpu_custom_call" | custom-call | tf_op jit(solution)/shard_map/pallas_call | solution.py:291
  (5 shorter events, 0.1 us)
Async XLA Ops:
  1.4 23.0 %collective-permute-start.2 = (bf16[4,3,32,128]{3,2,1,0:T(8,128)(2,1)S(1)}, bf16[4,3,32,128]{3,2,1,0:T(8,128)(2,1)S(1)}, u32[]{:S(2)}, u32[]{:S(2)}) collective-permute-start(bf16[4,3,32,128]{3,2,1,0:T(8,128)(2,1)S(1)} %reshape.102), channel_id=1, source_target_pairs={{0,48},{1,83},{16,64},{17,99},{32,80},{33,115},{48,96},{49,1},{64,... | collective-permute-start | bytes 294920 | tf_op jit(solution)/shard_map/ppermute | solution.py:177
  14.3 10.2 %collective-permute-start.1 = (bf16[4,3,32,128]{3,2,1,0:T(8,128)(2,1)S(1)}, bf16[4,3,32,128]{3,2,1,0:T(8,128)(2,1)S(1)}, u32[]{:S(2)}, u32[]{:S(2)}) collective-permute-start(bf16[4,3,32,128]{3,2,1,0:T(8,128)(2,1)S(1)} %reshape.102), channel_id=1, source_target_pairs={{0,32},{1,99},{16,48},{17,115},{32,64},{33,1},{48,80},{49,17},{64,... | collective-permute-start | bytes 294920 | tf_op jit(solution)/shard_map/ppermute | solution.py:177
  18.6 5.9 %collective-permute-start = (bf16[4,3,32,128]{3,2,1,0:T(8,128)(2,1)S(1)}, bf16[4,3,32,128]{3,2,1,0:T(8,128)(2,1)S(1)}, u32[]{:S(2)}, u32[]{:S(2)}) collective-permute-start(bf16[4,3,32,128]{3,2,1,0:T(8,128)(2,1)S(1)} %reshape.102), channel_id=1, source_target_pairs={{0,16},{1,115},{16,32},{17,1},{32,48},{33,17},{48,64},{49,33},{64,... | collective-permute-start | bytes 294920 | tf_op jit(solution)/shard_map/ppermute | solution.py:177
  24.5 34.4 %copy-start = (bf16[128,4096]{1,0:T(8,128)(2,1)S(1)}, bf16[128,4096]{1,0:T(8,128)(2,1)}, u32[]{:S(2)}) copy-start(bf16[128,4096]{1,0:T(8,128)(2,1)} %tokens_ref.3) | copy-start | bytes 3145732
  24.5 34.4 %copy-start.1 = (f32[4096]{0:T(1024)S(1)}, f32[4096]{0:T(1024)}, u32[]{:S(2)}) copy-start(f32[4096]{0:T(1024)} %param.7) | copy-start | bytes 49156
  24.5 10.8 %collective-permute-start.6 = (bf16[3,2,3,32,128]{4,3,2,1,0:T(8,128)(2,1)S(1)}, bf16[3,2,3,32,128]{4,3,2,1,0:T(8,128)(2,1)S(1)}, u32[]{:S(2)}, u32[]{:S(2)}) collective-permute-start(bf16[3,2,3,32,128]{4,3,2,1,0:T(8,128)(2,1)S(1)} %get-tuple-element.36), channel_id=1, source_target_pairs={{0,1},{1,0},{2,3},{3,2},{4,5},{5,4},{6,7},{7,6},{8,9},{9,8},{10,11... | collective-permute-start | bytes 442376 | tf_op jit(solution)/shard_map/ppermute | solution.py:191
  26.6 8.8 %collective-permute-start.5 = (bf16[2,3,32,128]{3,2,1,0:T(8,128)(2,1)S(1)}, bf16[2,3,32,128]{3,2,1,0:T(8,128)(2,1)S(1)}, u32[]{:S(2)}, u32[]{:S(2)}) collective-permute-start(bf16[2,3,32,128]{3,2,1,0:T(8,128)(2,1)S(1)} %get-tuple-element.38), channel_id=1, source_target_pairs={{0,64},{1,67},{16,80},{17,83},{32,96},{33,99},{48,112},{49,115},{6... | collective-permute-start | bytes 147464 | tf_op jit(solution)/shard_map/ppermute | solution.py:177
  35.5 10.7 %collective-permute-start.9 = (bf16[2,24,32,128]{3,2,1,0:T(8,128)(2,1)S(1)}, bf16[2,24,32,128]{3,2,1,0:T(8,128)(2,1)S(1)}, u32[]{:S(2)}, u32[]{:S(2)}) collective-permute-start(bf16[2,24,32,128]{3,2,1,0:T(8,128)(2,1)S(1)} %bitcast.27), channel_id=1, source_target_pairs={{0,4},{1,129},{4,8},{5,133},{8,12},{9,137},{12,0},{13,141},{128,13... | collective-permute-start | bytes 1179656 | tf_op jit(solution)/shard_map/ppermute | solution.py:187
  38.7 12.3 %collective-permute-start.8 = (bf16[2,24,32,128]{3,2,1,0:T(8,128)(2,1)S(1)}, bf16[2,24,32,128]{3,2,1,0:T(8,128)(2,1)S(1)}, u32[]{:S(2)}, u32[]{:S(2)}) collective-permute-start(bf16[2,24,32,128]{3,2,1,0:T(8,128)(2,1)S(1)} %bitcast.28), channel_id=1, source_target_pairs={{0,8},{1,257},{4,12},{5,261},{8,0},{9,265},{12,4},{13,269},{128,13... | collective-permute-start | bytes 1179656 | tf_op jit(solution)/shard_map/ppermute | solution.py:187
  43.2 9.1 %collective-permute-start.7 = (bf16[2,24,32,128]{3,2,1,0:T(8,128)(2,1)S(1)}, bf16[2,24,32,128]{3,2,1,0:T(8,128)(2,1)S(1)}, u32[]{:S(2)}, u32[]{:S(2)}) collective-permute-start(bf16[2,24,32,128]{3,2,1,0:T(8,128)(2,1)S(1)} %bitcast.29), channel_id=1, source_target_pairs={{0,12},{1,385},{4,0},{5,389},{8,4},{9,393},{12,8},{13,397},{128,14... | collective-permute-start | bytes 1179656 | tf_op jit(solution)/shard_map/ppermute | solution.py:187
  52.4 30.0 %collective-permute-start.11 = (bf16[96,32,128]{2,1,0:T(8,128)(2,1)S(1)}, bf16[96,32,128]{2,1,0:T(8,128)(2,1)S(1)}, u32[]{:S(2)}, u32[]{:S(2)}) collective-permute-start(bf16[96,32,128]{2,1,0:T(8,128)(2,1)S(1)} %get-tuple-element.30.refs_7_), channel_id=1, source_target_pairs={{0,128},{1,5},{4,132},{5,9},{8,136},{9,13},{12,140},{13,1},{128,25... | collective-permute-start | bytes 2359304 | tf_op jit(solution)/shard_map/ppermute | solution.py:187
  55.5 29.1 %collective-permute-start.13 = (bf16[96,32,128]{2,1,0:T(8,128)(2,1)S(1)}, bf16[96,32,128]{2,1,0:T(8,128)(2,1)S(1)}, u32[]{:S(2)}, u32[]{:S(2)}) collective-permute-start(bf16[96,32,128]{2,1,0:T(8,128)(2,1)S(1)} %get-tuple-element.31.refs_11_), channel_id=1, source_target_pairs={{0,384},{1,13},{4,388},{5,1},{8,392},{9,5},{12,396},{13,9},{128,0}... | collective-permute-start | bytes 2359304 | tf_op jit(solution)/shard_map/ppermute | solution.py:187
  59.5 35.7 %collective-permute-start.4 = (bf16[4096,128]{1,0:T(8,128)(2,1)S(1)}, bf16[4096,128]{1,0:T(8,128)(2,1)S(1)}, u32[]{:S(2)}, u32[]{:S(2)}) collective-permute-start(bf16[4096,128]{1,0:T(8,128)(2,1)S(1)} %get-tuple-element.26), channel_id=1, source_target_pairs={{0,1},{1,0},{2,3},{3,2},{4,5},{5,4},{6,7},{7,6},{8,9},{9,8},{10,11... | collective-permute-start | bytes 3145736 | tf_op jit(solution)/shard_map/ppermute | solution.py:191
  64.9 13.4 %collective-permute-start.3 = (f32[56,64]{1,0:T(8,128)S(1)}, f32[56,64]{1,0:T(8,128)S(1)}, u32[]{:S(2)}, u32[]{:S(2)}) collective-permute-start(f32[56,64]{1,0:T(8,128)S(1)} %reshape.107.near_ref), channel_id=1, source_target_pairs={{0,2},{2,0},{1,3},{3,1},{4,6},{6,4},{5,7},{7,5},{8,10},{10,8},{9,1... | collective-permute-start | bytes 43016 | tf_op jit(solution)/shard_map/ppermute | solution.py:350
  73.1 22.2 %collective-permute-start.10 = (bf16[96,32,128]{2,1,0:T(8,128)(2,1)S(1)}, bf16[96,32,128]{2,1,0:T(8,128)(2,1)S(1)}, u32[]{:S(2)}, u32[]{:S(2)}) collective-permute-start(bf16[96,32,128]{2,1,0:T(8,128)(2,1)S(1)} %get-tuple-element.30.refs_7_), channel_id=1, source_target_pairs={{0,384},{1,13},{4,388},{5,1},{8,392},{9,5},{12,396},{13,9},{128,0}... | collective-permute-start | bytes 2359304 | tf_op jit(solution)/shard_map/ppermute | solution.py:187
  78.4 16.9 %collective-permute-start.15 = (bf16[96,32,128]{2,1,0:T(8,128)(2,1)S(1)}, bf16[96,32,128]{2,1,0:T(8,128)(2,1)S(1)}, u32[]{:S(2)}, u32[]{:S(2)}) collective-permute-start(bf16[96,32,128]{2,1,0:T(8,128)(2,1)S(1)} %get-tuple-element.31.refs_11_), channel_id=1, source_target_pairs={{0,128},{1,5},{4,132},{5,9},{8,136},{9,13},{12,140},{13,1},{128,25... | collective-permute-start | bytes 2359304 | tf_op jit(solution)/shard_map/ppermute | solution.py:187
  82.4 18.6 %collective-permute-start.12 = (bf16[96,32,128]{2,1,0:T(8,128)(2,1)S(1)}, bf16[96,32,128]{2,1,0:T(8,128)(2,1)S(1)}, u32[]{:S(2)}, u32[]{:S(2)}) collective-permute-start(bf16[96,32,128]{2,1,0:T(8,128)(2,1)S(1)} %collective-permute-done.11.refs_10_), channel_id=1, source_target_pairs={{0,128},{1,5},{4,132},{5,9},{8,136},{9,13},{12,140},{13,1},{128,25... | collective-permute-start | bytes 2359304 | tf_op jit(solution)/shard_map/ppermute | solution.py:187
  84.7 16.4 %collective-permute-start.14 = (bf16[96,32,128]{2,1,0:T(8,128)(2,1)S(1)}, bf16[96,32,128]{2,1,0:T(8,128)(2,1)S(1)}, u32[]{:S(2)}, u32[]{:S(2)}) collective-permute-start(bf16[96,32,128]{2,1,0:T(8,128)(2,1)S(1)} %collective-permute-done.13.refs_12_), channel_id=1, source_target_pairs={{0,384},{1,13},{4,388},{5,1},{8,392},{9,5},{12,396},{13,9},{128,0}... | collective-permute-start | bytes 2359304 | tf_op jit(solution)/shard_map/ppermute | solution.py:187
  109.0 6.1 %collective-permute-start.16 = (bf16[64,64,128]{2,1,0:T(8,128)(2,1)S(1)}, bf16[64,64,128]{2,1,0:T(8,128)(2,1)S(1)}, u32[]{:S(2)}, u32[]{:S(2)}) collective-permute-start(bf16[64,64,128]{2,1,0:T(8,128)(2,1)S(1)} %get-tuple-element.33), channel_id=1, source_target_pairs={{0,1},{1,0},{2,3},{3,2},{4,5},{5,4},{6,7},{7,6},{8,9},{9,8},{10,11... | collective-permute-start | bytes 3145736 | tf_op jit(solution)/shard_map/ppermute | solution.py:191
